TPU v7x, 512 devices: a whole 4x4x16 slice. The times are simulated.
512 devices in a mesh: dom: 64 (over x, z), split: 8 (over y, core).
Axes of the slice: x: 4, y: 4, z: 16, core: 2. Of those that a mesh axis runs over, the one named last changes fastest.
Arguments:
- modes_now: float32 [64, 4096, 128], P('split', 'dom'), may hold values from -6 to 6
- modes_prev: float32 [64, 4096, 128], P('split', 'dom'), may hold values from -6 to 6
- z_extent: int32 [64], P('dom'), may hold values from 16 to 64, as said below
- lower_nbr: int32 [64], P('dom'), may hold values from -1 to 63, as said below
- upper_nbr: int32 [64], P('dom'), may hold values from -1 to 63
- x_shift: int32 [64, 2], P('dom'), may hold values from -32 to 32, as said below
- y_shift: int32 [64, 2], P('dom'), may hold values from -32 to 32, as said below
Outputs:
- modes_next: float32 [64, 4096, 128], P('split', 'dom')
- modes_cur: float32 [64, 4096, 128], P('split', 'dom')
- pressure: float32 [64, 4096, 128], P('split', 'dom')
Inputs may be any that keep to these rules, and one draw needn't show every extreme that they name: `z_extent`: at least one cuboid reaches the full 64 slots. Cuboids form chains: if upper_nbr[a] = b then lower_nbr[b] = a, and no cuboid is its own neighbour. If upper_nbr[a] = b then x_shift[a, 1] = -x_shift[b, 0]; zero at walls. If upper_nbr[a] = b then y_shift[a, 1] = -y_shift[b, 0]; zero at walls.
All inputs are finite; a program needn't handle non-finite values.
Results may differ from a plain program's by a relative error of at most 0.0003.
Values sent between devices are 32-bit elements; how exact they have to be, the bound alone decides.
A program may use at most 64 MiB of HBM per device.

v0:
```python
import jax
import jax.numpy as jnp
from jax import lax
from jax.sharding import PartitionSpec as P

STEPS = 2


HIGH = lax.Precision.HIGHEST
STENCIL = (-490.0 / 180.0, 270.0 / 180.0, -27.0 / 180.0, 2.0 / 180.0)
COURANT = 0.5


def cut_along(value, dim, length):
    shape = value.shape
    blocks = value.reshape(*shape[:dim], length, shape[dim] // length, *shape[dim + 1 :])
    return jnp.moveaxis(blocks, dim, 0)


def sent_and_summed(value, axis, dim):
    length = lax.axis_size(axis)
    blocks = lax.all_to_all(cut_along(value, dim, length), axis, 0, 0, tiled=True)
    return jnp.sum(blocks, axis=0)


def sent_together(arrays, axis, dim, along):
    both = jnp.concatenate(arrays, axis=along)
    out, at, done = (lax.all_gather(both, axis, axis=dim, tiled=True), 0, [])
    for a in arrays:
        done.append(lax.slice_in_dim(out, at, at + a.shape[along], axis=along))
        at += a.shape[along]
    return tuple(done)


def cosine_table(kk, xx, length):
    scale = jnp.where(kk == 0, jnp.sqrt(1.0 / length), jnp.sqrt(2.0 / length))
    return scale * jnp.cos(jnp.pi * kk * (xx + 0.5) / length)


def shifted(face, rows, move_y):
    count = face.shape[0]
    width = face.shape[2]
    cols = jnp.arange(width) + move_y
    rows_ok = (rows >= 0) & (rows < count)
    cols_ok = (cols >= 0) & (cols < width)
    picked = jnp.take(face, jnp.clip(rows, 0, count - 1), axis=0)
    picked = jnp.take(picked, jnp.clip(cols, 0, width - 1), axis=2)
    mask = (rows_ok[:, None, None] & cols_ok[None, None, :]).astype(jnp.float32)
    return (picked, mask)


def along_x(values, forward):
    slab = values.shape[0]
    full = slab * lax.axis_size("split")
    offset = lax.axis_index("split") * slab
    outer = jnp.arange(slab * lax.axis_size("split")).astype(jnp.float32)[:, None]
    inner = (offset + jnp.arange(slab)).astype(jnp.float32)[None, :]
    if forward:
        table = cosine_table(outer, inner, jnp.float32(full))
    else:
        table = cosine_table(inner, outer, jnp.float32(full))
    return sent_and_summed(
        jnp.dot(table, values, precision=HIGH, preferred_element_type=jnp.float32), "split", 0
    )


def neighbours(lower_face, upper_face, below, above):
    slots = jnp.arange(lax.axis_size("dom"))
    to_upper = (slots == above).astype(jnp.float32)[:, None, None, None]
    to_lower = (slots == below).astype(jnp.float32)[:, None, None, None]
    outgoing = jnp.stack([to_upper * upper_face[None], to_lower * lower_face[None]], axis=1)
    incoming = lax.all_to_all(outgoing, "dom", split_axis=0, concat_axis=0, tiled=True)
    summed = jnp.sum(incoming, axis=0)
    return (summed[0], summed[1])


def interface(lower_face, upper_face, from_lower, from_upper, has_lower, has_upper):
    low_rows = []
    for jj in range(3):
        total = jnp.zeros_like(lower_face[:, 0, :])
        for mm in range(-3, 0):
            if abs(jj - mm) <= 3:
                total = total + STENCIL[abs(jj - mm)] * (
                    from_lower[:, mm + 3, :] - lower_face[:, -1 - mm, :]
                )
        low_rows.append(total)
    up_rows = []
    for aa in range(3):
        tt = aa - 3
        total = jnp.zeros_like(upper_face[:, 0, :])
        for mm in range(3):
            if abs(tt - mm) <= 3:
                total = total + STENCIL[abs(tt - mm)] * (
                    from_upper[:, mm, :] - upper_face[:, 2 - mm, :]
                )
        up_rows.append(total)
    low = jnp.stack(low_rows, axis=1) * has_lower
    upp = jnp.stack(up_rows, axis=1) * has_upper
    return COURANT**2 * jnp.concatenate([low, upp], axis=1)


def on_device(modes_now, modes_prev, z_extent, lower_nbr, upper_nbr, x_shift, y_shift):
    slab, zcap, width = modes_now.shape
    full = slab * lax.axis_size("split")
    extent = z_extent[0]
    lenf = extent.astype(jnp.float32)
    zidx = jnp.arange(zcap)
    live = zidx < extent
    kz = zidx.astype(jnp.float32)
    ztable = jnp.where(
        live[:, None] & live[None, :], cosine_table(kz[:, None], kz[None, :], lenf), 0.0
    )
    rows = jnp.array([0, 1, 2, -3, -2, -1], jnp.int32) + jnp.where(jnp.arange(6) >= 3, extent, 0)
    onerow = (zidx[None, :] == rows[:, None]).astype(jnp.float32)
    row_table = jnp.dot(ztable, onerow.T, precision=HIGH, preferred_element_type=jnp.float32)
    yindex = jnp.arange(width).astype(jnp.float32)
    ytable = cosine_table(yindex[:, None], yindex[None, :], jnp.float32(width))
    own_rows = lax.axis_index("split") * slab + jnp.arange(slab)
    kx = own_rows.astype(jnp.float32)
    freq = (
        COURANT
        * jnp.pi
        * jnp.sqrt(
            (kx / full)[:, None, None] ** 2
            + (kz / lenf)[None, :, None] ** 2
            + (yindex / width)[None, None, :] ** 2
        )
    )
    twice_cos = 2.0 * jnp.cos(freq)
    gain = jnp.sinc(freq / (2.0 * jnp.pi)) ** 2
    below = lower_nbr[0]
    above = upper_nbr[0]
    has_lower = (below >= 0).astype(jnp.float32)
    has_upper = (above >= 0).astype(jnp.float32)
    keep = live.astype(jnp.float32)[None, :, None]
    current = modes_now * keep
    older = modes_prev * keep
    for step in range(STEPS):
        strip = jnp.einsum(
            "kr,xky->xry", row_table, current, precision=HIGH, preferred_element_type=jnp.float32
        )
        strip = jnp.einsum(
            "xrk,ky->xry", strip, ytable, precision=HIGH, preferred_element_type=jnp.float32
        )
        strip = along_x(strip.reshape(slab, 6 * width), False).reshape(slab, 6, width)
        lower_face = strip[:, 0:3]
        upper_face = strip[:, 3:6]
        got_lower, got_upper = neighbours(lower_face, upper_face, below, above)
        whole_lower, whole_upper = sent_together((got_lower, got_upper), "split", 0, 1)
        from_lower, mask_low = shifted(whole_lower, own_rows + x_shift[0, 0], y_shift[0, 0])
        from_upper, mask_up = shifted(whole_upper, own_rows + x_shift[0, 1], y_shift[0, 1])
        forcing = interface(
            lower_face,
            upper_face,
            from_lower,
            from_upper,
            has_lower * mask_low,
            has_upper * mask_up,
        )
        forced = jnp.einsum(
            "xry,ky->xrk", forcing, ytable, precision=HIGH, preferred_element_type=jnp.float32
        )
        forced = along_x(forced.reshape(slab, 6 * width), True).reshape(slab, 6, width)
        fmodes = jnp.einsum(
            "kr,xry->xky", row_table, forced, precision=HIGH, preferred_element_type=jnp.float32
        )
        newer = twice_cos * current - older + gain * fmodes
        older, current = (current, newer)
    field = jnp.einsum(
        "kz,xky->xzy", ztable, current, precision=HIGH, preferred_element_type=jnp.float32
    )
    field = jnp.einsum(
        "xzk,ky->xzy", field, ytable, precision=HIGH, preferred_element_type=jnp.float32
    )
    xindex = jnp.arange(full).astype(jnp.float32)
    xtable = cosine_table(xindex[:, None], xindex[None, :], jnp.float32(full))
    wide = jnp.einsum(
        "kx,kzy->xzy",
        xtable,
        lax.all_to_all(field, "split", split_axis=1, concat_axis=0, tiled=True),
        precision=HIGH,
        preferred_element_type=jnp.float32,
    )
    pressure = lax.all_to_all(wide, "split", split_axis=0, concat_axis=1, tiled=True)
    return (current, older, pressure)


def solution(mesh):
    placed = (
        P("split", "dom", None),
        P("split", "dom", None),
        P("dom"),
        P("dom"),
        P("dom"),
        P("dom", None),
        P("dom", None),
    )
    return jax.shard_map(
        on_device,
        mesh=mesh,
        in_specs=placed,
        out_specs=(P("split", "dom", None), P("split", "dom", None), P("split", "dom", None)),
        check_vma=False,
    )
```

profile of v0, /device:TPU:1, one launch (start us, length us, event | category | flops | bytes accessed | tf_op | source)
XLA Modules:
  0.0 289.4 jit_solution(16149631394481077374)
XLA Ops:
  1.5 0.7 fusion.119
  2.5 1.3 convolution_bitcast_fusion.4
  4.3 1.2 fusion.60
  5.4 10.1 %all-to-all-start = ((f32[8,8,768]{2,1,0:T(8,128)}), f32[8,8,768]{2,1,0:T(8,128)S(1)}, u32[]{:S(2)}, u32[]{:S(2)}) async-start(f32[8,8,768]{2,1,0:T(8,128)} %fusion.60), calls=%async_computation | async-start | bytes 393216 | tf_op jit(solution)/shard_map/all_to_all | solution.py:22
  16.9 4.6 %all-to-all-done = f32[8,8,768]{2,1,0:T(8,128)S(1)} async-done(((f32[8,8,768]{2,1,0:T(8,128)}), f32[8,8,768]{2,1,0:T(8,128)S(1)}, u32[]{:S(2)}, u32[]{:S(2)}) %all-to-all-start) | async-done | bytes 196640 | tf_op jit(solution)/shard_map/all_to_all | solution.py:22
  21.8 1.3 pad_maximum_fusion
  23.0 14.2 %all-to-all-start.1 = ((f32[64,2,8,3,128]{4,2,3,1,0:T(8,128)}), f32[64,2,8,3,128]{4,2,3,1,0:T(8,128)S(1)}, u32[]{:S(2)}, u32[]{:S(2)}) async-start(f32[64,2,8,3,128]{4,2,3,1,0:T(8,128)} %pad_maximum_fusion), calls=%async_computation.1 | async-start | bytes 3145728 | tf_op jit(solution)/shard_map/all_to_all | solution.py:72
  38.5 0.7 compare_and_fusion.2
  39.2 0.7 compare_and_fusion.6
  40.5 0.7 compare_and_fusion
  42.5 1.3 compare_and_fusion.5
  43.8 1.3 compare_and_fusion.1
  45.3 62.4 %all-to-all-done.1 = f32[64,2,8,3,128]{4,2,3,1,0:T(8,128)S(1)} async-done(((f32[64,2,8,3,128]{4,2,3,1,0:T(8,128)}), f32[64,2,8,3,128]{4,2,3,1,0:T(8,128)S(1)}, u32[]{:S(2)}, u32[]{:S(2)}) %all-to-all-start.1) | async-done | bytes 1572896 | tf_op jit(solution)/shard_map/all_to_all | solution.py:72
  107.8 19.3 %all_gather.6 = f32[64,6,128]{2,0,1:T(8,128)S(1)} all-gather(f32[8,6,128]{2,0,1:T(8,128)S(1)} %pad_maximum_fusion.2), channel_id=1, replica_groups=mesh['dom'=64,'split'=8] {'split'}, dimensions={0}, use_global_device_ids=true | all-gather | bytes 221184 | tf_op jit(solution)/shard_map/all_gather | solution.py:28
  128.0 0.7 gather_fusion.1
  129.8 0.8 gather_fusion.3
  131.2 1.2 fusion.62
  132.4 3.5 %all-to-all-start.2 = ((f32[8,8,768]{2,1,0:T(8,128)}), f32[8,8,768]{2,1,0:T(8,128)S(1)}, u32[]{:S(2)}, u32[]{:S(2)}) async-start(f32[8,8,768]{2,1,0:T(8,128)} %fusion.62), calls=%async_computation.2 | async-start | bytes 393216 | tf_op jit(solution)/shard_map/all_to_all | solution.py:22
  135.9 5.8 %all-to-all-done.2 = f32[8,8,768]{2,1,0:T(8,128)S(1)} async-done(((f32[8,8,768]{2,1,0:T(8,128)}), f32[8,8,768]{2,1,0:T(8,128)S(1)}, u32[]{:S(2)}, u32[]{:S(2)}) %all-to-all-start.2) | async-done | bytes 196640 | tf_op jit(solution)/shard_map/all_to_all | solution.py:22
  141.8 1.6 fusion.3
  144.6 9.2 %all_to_all.66 = f32[8,8,768]{2,1,0:T(8,128)S(1)} all-to-all(f32[8,8,768]{2,1,0:T(8,128)S(1)} %fusion.59), channel_id=1, replica_groups=mesh['dom'=64,'split'=8] {'split'}, dimensions={0} | all-to-all | bytes 393216 | tf_op jit(solution)/shard_map/all_to_all | solution.py:22
  154.2 77.0 %all_to_all.67 = f32[64,2,8,3,128]{4,2,3,1,0:T(8,128)S(1)} all-to-all(f32[64,2,8,3,128]{4,2,3,1,0:T(8,128)S(1)} %pad_maximum_fusion.1), channel_id=1, replica_groups=mesh['dom'=64,'split'=8] {'dom'}, dimensions={0} | all-to-all | bytes 3145728 | tf_op jit(solution)/shard_map/all_to_all | solution.py:72
  231.3 19.3 %all_gather.7 = f32[64,6,128]{2,0,1:T(8,128)S(1)} all-gather(f32[8,6,128]{2,0,1:T(8,128)S(1)} %pad_maximum_fusion.3), channel_id=1, replica_groups=mesh['dom'=64,'split'=8] {'split'}, dimensions={0}, use_global_device_ids=true | all-gather | bytes 221184 | tf_op jit(solution)/shard_map/all_gather | solution.py:28
  251.5 0.7 gather_fusion.5
  253.2 0.8 gather_fusion.7
  255.2 8.6 %all_to_all.68 = f32[8,8,768]{2,1,0:T(8,128)S(1)} all-to-all(f32[8,8,768]{2,1,0:T(8,128)S(1)} %fusion.61), channel_id=1, replica_groups=mesh['dom'=64,'split'=8] {'split'}, dimensions={0} | all-to-all | bytes 393216 | tf_op jit(solution)/shard_map/all_to_all | solution.py:22
  263.8 1.5 fusion.1
  265.9 1.5 fusion.14
  267.3 4.3 %all-to-all-start.6 = ((f32[8,64,128]{2,0,1:T(8,128)}), f32[8,64,128]{2,0,1:T(8,128)S(1)}, u32[]{:S(2)}, u32[]{:S(2)}) async-start(f32[8,64,128]{2,0,1:T(8,128)} %fusion.14), calls=%async_computation.6 | async-start | bytes 524288 | tf_op jit(solution)/shard_map/all_to_all | solution.py:180
  271.6 6.5 %all-to-all-done.6 = f32[8,64,128]{2,0,1:T(8,128)S(1)} async-done(((f32[8,64,128]{2,0,1:T(8,128)}), f32[8,64,128]{2,0,1:T(8,128)S(1)}, u32[]{:S(2)}, u32[]{:S(2)}) %all-to-all-start.6) | async-done | bytes 262176 | tf_op jit(solution)/shard_map/all_to_all | solution.py:180
  278.8 9.9 %all_to_all.69 = f32[64,8,128]{2,1,0:T(8,128)S(1)} all-to-all(f32[64,8,128]{2,1,0:T(8,128)S(1)} %copy.65), channel_id=1, replica_groups=mesh['dom'=64,'split'=8] {'split'}, dimensions={0} | all-to-all | bytes 524288 | tf_op jit(solution)/shard_map/all_to_all | solution.py:184
  288.7 0.7 copy.88
  (101 shorter events, 13.2 us)
Async XLA Ops:
  5.4 16.0 %all-to-all-start = ((f32[8,8,768]{2,1,0:T(8,128)}), f32[8,8,768]{2,1,0:T(8,128)S(1)}, u32[]{:S(2)}, u32[]{:S(2)}) async-start(f32[8,8,768]{2,1,0:T(8,128)} %fusion.60), calls=%async_computation | async-start | bytes 393216 | tf_op jit(solution)/shard_map/all_to_all | solution.py:22
  23.0 14.2 %copy-start.3 = (s32[1,2]{1,0:T(1,128)S(1)}, s32[1,2]{1,0:T(1,128)}, u32[]{:S(2)}) copy-start(s32[1,2]{1,0:T(1,128)} %param.18) | copy-start | bytes 28
  23.0 18.8 %copy-start.4 = (s32[1,2]{1,0:T(1,128)S(1)}, s32[1,2]{1,0:T(1,128)}, u32[]{:S(2)}) copy-start(s32[1,2]{1,0:T(1,128)} %param.17) | copy-start | bytes 28
  23.0 84.6 %all-to-all-start.1 = ((f32[64,2,8,3,128]{4,2,3,1,0:T(8,128)}), f32[64,2,8,3,128]{4,2,3,1,0:T(8,128)S(1)}, u32[]{:S(2)}, u32[]{:S(2)}) async-start(f32[64,2,8,3,128]{4,2,3,1,0:T(8,128)} %pad_maximum_fusion), calls=%async_computation.1 | async-start | bytes 3145728 | tf_op jit(solution)/shard_map/all_to_all | solution.py:72
  127.1 14.7 %copy-start = (f32[8,64,128]{2,1,0:T(8,128)S(1)}, f32[8,64,128]{2,1,0:T(8,128)}, u32[]{:S(2)}) copy-start(f32[8,64,128]{2,1,0:T(8,128)} %param.12) | copy-start | bytes 786436
  127.1 14.7 %copy-start.5 = (f32[8,64,128]{2,1,0:T(8,128)S(1)}, f32[8,64,128]{2,1,0:T(8,128)}, u32[]{:S(2)}) copy-start(f32[8,64,128]{2,1,0:T(8,128)} %param.13) | copy-start | bytes 786436
  132.4 9.3 %all-to-all-start.2 = ((f32[8,8,768]{2,1,0:T(8,128)}), f32[8,8,768]{2,1,0:T(8,128)S(1)}, u32[]{:S(2)}, u32[]{:S(2)}) async-start(f32[8,8,768]{2,1,0:T(8,128)} %fusion.62), calls=%async_computation.2 | async-start | bytes 393216 | tf_op jit(solution)/shard_map/all_to_all | solution.py:22
  143.3 120.4 %copy-start.1 = (f32[8,64,128]{2,1,0:T(8,128)}, f32[8,64,128]{2,1,0:T(8,128)S(1)}, u32[]{:S(2)}) copy-start(f32[8,64,128]{2,1,0:T(8,128)S(1)} %fusion.3) | copy-start | bytes 786436
  265.3 23.4 %copy-start.2 = (f32[8,64,128]{2,1,0:T(8,128)}, f32[8,64,128]{2,1,0:T(8,128)S(1)}, u32[]{:S(2)}) copy-start(f32[8,64,128]{2,1,0:T(8,128)S(1)} %fusion.1) | copy-start | bytes 786436
  267.3 10.8 %all-to-all-start.6 = ((f32[8,64,128]{2,0,1:T(8,128)}), f32[8,64,128]{2,0,1:T(8,128)S(1)}, u32[]{:S(2)}, u32[]{:S(2)}) async-start(f32[8,64,128]{2,0,1:T(8,128)} %fusion.14), calls=%async_computation.6 | async-start | bytes 524288 | tf_op jit(solution)/shard_map/all_to_all | solution.py:180
where the time goes:
time: 290 us; the launch traced here: 289 us
  blocking collectives  143 us (49%)
  waiting for transfers between devices  79.2 us (27%)
  starting transfers between devices  32.1 us (11%)
  matrix products  12.7 us (4%)
  other arithmetic  10.2 us (4%)
  local copies, waits for them, and re-layouts  8.67 us (3%)
  between operations  3.33 us (1%)
    all_to_all x1, blocking collectives, neighbours(): lax.all_to_all(outgoing, 'dom', split_axis=0, concat_axis=0, tiled=True)  77 us
    all_to_all x1, waiting for transfers between devices, neighbours(): lax.all_to_all(outgoing, 'dom', split_axis=0, concat_axis=0, tiled=True)  62.4 us
    all_gather x2, blocking collectives, sent_together(): out, at, done = (lax.all_gather(both, axis, axis=dim, tiled=True), 0, [])  38.5 us
    all_to_all x2, blocking collectives, sent_and_summed(): lax.all_to_all(cut_along(value, dim, length), axis, 0, 0, tiled=True)  17.8 us
    all_to_all x1, starting transfers between devices, neighbours(): lax.all_to_all(outgoing, 'dom', split_axis=0, concat_axis=0, tiled=True)  14.2 us
    all_to_all x2, starting transfers between devices, sent_and_summed(): lax.all_to_all(cut_along(value, dim, length), axis, 0, 0, tiled=True)  13.6 us
    all_to_all x2, waiting for transfers between devices, sent_and_summed(): lax.all_to_all(cut_along(value, dim, length), axis, 0, 0, tiled=True)  10.4 us
    all_to_all x1, blocking collectives, on_device(): lax.all_to_all(wide, 'split', split_axis=0, concat_axis=1, tiled=True)  9.91 us
  transfers between devices with their start and end apart: 4, of which 4 were waited for; matrix products, arithmetic and copies ran while one was open for 3% of the time, Pallas kernels for 0%

commit v1 on v0

v1 whole, which is shorter than its diff:
```python
import functools
import math

import jax
import jax.numpy as jnp
import numpy as np
from jax import lax
from jax.experimental import pallas as pl
from jax.experimental.pallas import tpu as pltpu
from jax.sharding import PartitionSpec as P

F32 = jnp.float32
HIGH = lax.Precision.HIGHEST
XN, ZN, SN = 4, 16, 8
NX, NY, ZC = 64, 128, 64
QUARTER = 0.25
ST1, ST2, ST3 = 270.0 / 180.0, -27.0 / 180.0, 2.0 / 180.0
GAIN = [2.0 * (-1.0) ** n / math.factorial(2 * n + 2) for n in range(12)]
HALF_PI_2 = (math.pi / 2) ** 2


def dot(a, b):
    return jnp.dot(a, b, precision=HIGH, preferred_element_type=F32)


def dot_nt(a, b):
    return lax.dot_general(a, b, (((1,), (1,)), ((), ())), precision=HIGH, preferred_element_type=F32)


def gain_of(u):
    g = jnp.full(u.shape, GAIN[-1], F32)
    for c in GAIN[-2::-1]:
        g = g * u + c
    return g


def cos_table(k, x, length):
    n = k * (2.0 * x + 1.0)
    period = 4.0 * length
    rest = n - period * jnp.floor(n / period + 0.5)
    w = (math.pi / 2) * (rest / length)
    u = w * w
    scale = jnp.where(k == 0, jnp.sqrt(1.0 / length), jnp.sqrt(2.0 / length))
    return scale * (1.0 - 0.5 * u * gain_of(u))


def iota(shape, dim):
    return lax.broadcasted_iota(jnp.int32, shape, dim).astype(F32)


def low_rows(q1, q2, q3):
    return [ST1 * q1 + ST2 * q2 + ST3 * q3, ST2 * q1 + ST3 * q2, ST3 * q1]


def kernel(
    ext, low, upp, xs, ys, m0, m1, cx, cxt, cy,
    nxt, cur, prs,
    rt, rtt, ztt, mz, b1, gn, tc, h0, sscr, st, nb, near, sel, far, ab, xab, yab, g, hs, hb, e1, ge, yo, yr,
    nb_s, nb_r, near_s, near_r, far_s, far_r, ab_s, ab_r, h_s, h_r, y_s, y_r,
):
    dom, me = lax.axis_index("dom"), lax.axis_index("split")
    px, pz = dom // ZN, lax.rem(dom, ZN)

    def at(dx, dz):
        return lax.rem(px + dx + XN, XN) * ZN + lax.rem(pz + dz + ZN, ZN)

    def other(t):
        return lax.rem(me + t, SN)

    near_all = [(i, d) for i in range(XN) for d in range(-2, 3)]
    near_out = [p for p in near_all if p != (0, 0)]

    barrier = pltpu.get_barrier_semaphore()

    def greet(d, s):
        pl.semaphore_signal(barrier, inc=1, device_id=(d, s), device_id_type=pl.DeviceIdType.MESH)

    for i, d in near_out:
        greet(at(i, d), me)
    for k in range(1, 4):
        greet(at(0, 4 * k), me)
    for t in range(1, SN):
        greet(dom, other(t))

    started = []

    def send(src, dst, ss, rs, d, s):
        c = pltpu.make_async_remote_copy(
            src_ref=src, dst_ref=dst, send_sem=ss, recv_sem=rs, device_id=(d, s), device_id_type=pl.DeviceIdType.MESH
        )
        c.start()
        started.append(c)

    def arrived(dst, ss, rs):
        pltpu.make_async_remote_copy(
            src_ref=dst, dst_ref=dst, send_sem=ss, recv_sem=rs, device_id=(dom, me), device_id_type=pl.DeviceIdType.MESH
        ).wait_recv()

    length = ext[0].astype(F32)
    lowf, uppf = low[0].astype(F32), upp[0].astype(F32)

    def row_of(r):
        return jnp.where(r < 3, r, r + (length - 6.0))

    k8, r8 = iota((8, ZC), 1), iota((8, ZC), 0)
    rtt[...] = jnp.where((k8 < length) & (r8 < 6), cos_table(k8, row_of(r8), jnp.full((8, ZC), length)), 0.0)
    k8, r8 = iota((ZC, 8), 0), iota((ZC, 8), 1)
    rt[...] = jnp.where((k8 < length) & (r8 < 6), cos_table(k8, row_of(r8), jnp.full((ZC, 8), length)), 0.0)

    def rows(i):
        return pl.ds(pl.multiple_of(i * ZC, ZC), ZC)

    kz = iota((ZC, NY), 0)
    live = kz < length

    def first(i, _):
        m = jnp.where(live, m0[rows(i), :], 0.0)
        mz[rows(i), :] = m
        sscr[pl.ds(pl.multiple_of(i * 8, 8), 8), :] = dot(rtt[...], m)
        return 0

    lax.fori_loop(0, 8, first, 0)

    def put_strip(step):
        for r in range(6):
            st[step, r] = sscr[pl.ds(r, 8, stride=8), :]

    put_strip(0)
    nb[0, 0] = jnp.full((8, 128), lowf)
    nb[0, 1] = jnp.full((8, 128), uppf)
    pl.semaphore_wait(barrier, len(near_out) + 3 + SN - 1)

    def half(d):
        return slice(3, 6) if d == 2 else slice(0, 3) if d == -2 else slice(0, 6)

    def send_near(step):
        for n, (i, d) in enumerate(near_all):
            if (i, d) == (0, 0):
                continue
            h = half(d)
            send(st.at[step, h], near.at[step, n, h], near_s.at[step, n], near_r.at[step, n], at(i, d), me)

    for k in range(1, 4):
        send(nb.at[0], nb.at[k], nb_s.at[k], nb_r.at[k], at(0, -4 * k), me)
    send_near(0)

    def matrices(c, n, move):
        row, col = iota((n, n), 0), iota((n, n), 1)
        put = (col == row + move).astype(F32)
        table = c[...]
        seen = ((col + move >= 0) & (col + move < n)).astype(F32)
        return dot_nt(dot(table, put), table), dot_nt(table * seen, table)

    for f in range(2):
        has = jnp.where(jnp.full((NX, NX), uppf if f else lowf) >= 0, QUARTER, 0.0)
        a, b = matrices(cx, NX, xs[0, f].astype(F32))
        xab[f, :, 0:NX] = a * has
        xab[f, :, NX : 2 * NX] = -b * has
        a, b = matrices(cy, NY, ys[0, f].astype(F32))
        yab[f, 0] = a
        yab[f, 1] = b

    lv = jnp.full((ZC, NY), length)
    flat = kz / lv
    flat = flat * flat + (iota((ZC, NY), 1) / NY) ** 2

    def second(i, _):
        kx = (me * 8 + i).astype(F32) / NX
        u = HALF_PI_2 * (flat + kx * kx)
        gain = gain_of(u)
        tw = 2.0 - u * gain
        m = mz[rows(i), :]
        base = tw * m - jnp.where(live, m1[rows(i), :], 0.0)
        gn[rows(i), :] = gain
        tc[rows(i), :] = tw
        b1[rows(i), :] = base
        h0[rows(i), :] = tw * base - m
        return 0

    lax.fori_loop(0, 8, second, 0)

    def turn(k, _):
        hs[k] = h0[pl.ds(k, 8, stride=ZC), :]
        return 0

    lax.fori_loop(0, ZC, turn, 0)

    def send_ab(step, w):
        for t in range(1, SN):
            send(ab.at[step, w, me], ab.at[step, w, me], ab_s.at[step, w, t], ab_r.at[step, w, t], dom, other(t))

    def put_ab(step, w, lo, up):
        ab[step, w, me, 0:3] = dot_nt(jnp.concatenate(lo, axis=0), yab[0, w]).reshape(3, 8, NY)
        ab[step, w, me, 3:6] = dot_nt(jnp.concatenate(up, axis=0), yab[1, w]).reshape(3, 8, NY)
        send_ab(step, w)

    def own_part(step):
        p = [st[step, r] for r in range(6)]
        put_ab(step, 1, low_rows(p[0], p[1], p[2]), low_rows(p[5], p[4], p[3])[::-1])

    def exchange(step):
        lo = [[jnp.zeros((8, NY), F32)] * 3 for _ in range(4)]
        up = [[jnp.zeros((8, NY), F32)] * 3 for _ in range(4)]
        for n, (i, d) in enumerate(near_all):
            if (i, d) == (0, 0):
                block = st.at[step]
            else:
                h = half(d)
                arrived(near.at[step, n, h], near_s.at[step, n], near_r.at[step, n])
                block = near.at[step, n]
            who = at(-i, -d).astype(F32)
            if d >= -1:
                b = [block[r] for r in range(3, 6)]
                for k in range(4):
                    hit = nb[k, 0] == who
                    lo[k] = [jnp.where(hit, v, a) for v, a in zip(b, lo[k])]
            if d <= 1:
                b = [block[r] for r in range(3)]
                for k in range(4):
                    hit = nb[k, 1] == who
                    up[k] = [jnp.where(hit, v, a) for v, a in zip(b, up[k])]
        for k in range(1, 4):
            for r in range(3):
                sel[step, k, r] = lo[k][r]
                sel[step, k, r + 3] = up[k][r]
            send(sel.at[step, k], far.at[step, k], far_s.at[step, k], far_r.at[step, k], at(0, 4 * k), me)
        q = lo[0] + up[0]
        for k in range(1, 4):
            arrived(far.at[step, k], far_s.at[step, k], far_r.at[step, k])
            q = [a + far[step, k, r] for r, a in enumerate(q)]
        put_ab(step, 0, low_rows(q[2], q[1], q[0]), low_rows(q[3], q[4], q[5])[::-1])
        for t in range(1, SN):
            src = other(SN - t)
            for w in range(2):
                arrived(ab.at[step, w, src], ab_s.at[step, w, t], ab_r.at[step, w, t])
        for r in range(6):
            rhs = jnp.concatenate([ab[step, w, :, r].reshape(NX, NY) for w in range(2)], axis=0)
            g[step, r * NX : (r + 1) * NX, :] = dot(xab[r // 3], rhs)
        g[step, 6 * NX :, :] = jnp.zeros((2 * NX, NY), F32)

    def forced(step, i):
        return gn[rows(i), :] * dot(rt[...], g[step, pl.ds(me * 8 + i, 8, stride=NX), :])

    own_part(0)
    for t in range(1, SN):
        dst = pl.multiple_of(other(t) * 8, 8)
        send(hs.at[pl.ds(dst, 8)], hb.at[me], h_s.at[t], h_r.at[t], dom, other(t))
    hb[me] = hs[pl.ds(pl.multiple_of(me * 8, 8), 8)]
    kk, zz = iota((ZC, ZC), 1), iota((ZC, ZC), 0)
    ztt[...] = jnp.where((kk < length) & (zz < length), cos_table(kk, zz, jnp.full((ZC, ZC), length)), 0.0)
    for k in range(1, 4):
        arrived(nb.at[k], nb_s.at[k], nb_r.at[k])
    exchange(0)

    def step_one(i, _):
        m = b1[rows(i), :] + forced(0, i)
        cur[rows(i), :] = m
        sscr[pl.ds(pl.multiple_of(i * 8, 8), 8), :] = dot(rtt[...], m)
        return 0

    lax.fori_loop(0, 8, step_one, 0)
    put_strip(1)
    send_near(1)
    own_part(1)

    for t in range(1, SN):
        arrived(hb.at[other(SN - t)], h_s.at[t], h_r.at[t])
    kx2 = (iota((NX, NY), 0) / NX) ** 2 + (iota((NX, NY), 1) / NY) ** 2

    def rowsum(step, j):
        c = rt[pl.ds(me * 8 + j, 1), :]
        total = c[:, 0:1] * g[step, 0:NX, :]
        for r in range(1, 6):
            total = total + c[:, r : r + 1] * g[step, r * NX : (r + 1) * NX, :]
        return total

    def early(j, _):
        z = jnp.full((NX, NY), (me * 8 + j).astype(F32)) / lv
        u = HALF_PI_2 * (kx2 + z * z)
        gain = gain_of(u)
        ge[j] = gain
        e1[j] = hb[:, j].reshape(NX, NY) + gain * (2.0 - u * gain) * rowsum(0, j)
        return 0

    lax.fori_loop(0, 8, early, 0)
    exchange(1)

    def late(j, _):
        out = dot(cxt[...], e1[j] + ge[j] * rowsum(1, j))
        yo[:, j] = out.reshape(SN, 8, NY)
        return 0

    lax.fori_loop(0, 8, late, 0)
    mine = pl.ds(pl.multiple_of(me * 64, 64), 64)
    for t in range(1, SN):
        send(yo.at[other(t)], yr.at[me], y_s.at[t], y_r.at[t], dom, other(t))
    yr[me] = yo[me]

    def step_two(i, _):
        nxt[rows(i), :] = tc[rows(i), :] * cur[rows(i), :] - mz[rows(i), :] + forced(1, i)
        return 0

    lax.fori_loop(0, 8, step_two, 0)
    for t in range(1, SN):
        arrived(yr.at[other(SN - t)], y_s.at[t], y_r.at[t])

    for i in range(8):
        y = yr[:, :, i].reshape(ZC, NY)
        prs[i * ZC : (i + 1) * ZC, :] = dot(dot(ztt[...], y), cy[...])

    for c in started:
        c.wait_send()


def table(n):
    k, x = np.arange(n)[:, None], np.arange(n)[None, :]
    return (np.where(k == 0, math.sqrt(1 / n), math.sqrt(2 / n)) * np.cos(math.pi * k * (x + 0.5) / n)).astype(np.float32)


def on_device(modes_now, modes_prev, z_extent, lower_nbr, upper_nbr, x_shift, y_shift):
    slab = modes_now.shape[0]
    flat = jax.ShapeDtypeStruct((slab * ZC, NY), F32)
    cx = table(NX)
    smem, vmem = pl.BlockSpec(memory_space=pltpu.SMEM), pl.BlockSpec(memory_space=pltpu.VMEM)
    v = lambda *s: pltpu.VMEM(s, F32)
    dma = pltpu.SemaphoreType.DMA
    outs = pl.pallas_call(
        kernel,
        out_shape=(flat,) * 3,
        in_specs=[smem] * 5 + [vmem] * 5,
        out_specs=(vmem,) * 3,
        scratch_shapes=[
            v(ZC, 8), v(8, ZC), v(ZC, ZC),
            v(512, NY), v(512, NY), v(512, NY), v(512, NY), v(512, NY), v(64, NY),
            v(2, 6, 8, NY), v(4, 2, 8, NY), v(2, 20, 6, 8, NY), v(2, 4, 6, 8, NY), v(2, 4, 6, 8, NY),
            v(2, 2, 8, 6, 8, NY), v(2, NX, 2 * NX), v(2, 2, NY, NY), v(2, 8 * NX, NY),
            v(ZC, 8, NY), v(8, 8, 8, NY), v(8, NX, NY), v(8, NX, NY), v(8, 8, 8, NY), v(8, 8, 8, NY),
            dma((4,)), dma((4,)), dma((2, 20)), dma((2, 20)), dma((2, 4)), dma((2, 4)),
            dma((2, 2, 8)), dma((2, 2, 8)), dma((8,)), dma((8,)), dma((8,)), dma((8,)),
        ],
        compiler_params=pltpu.CompilerParams(collective_id=0, has_side_effects=True),
    )(
        z_extent, lower_nbr, upper_nbr, x_shift, y_shift,
        modes_now.reshape(slab * ZC, NY), modes_prev.reshape(slab * ZC, NY),
        jnp.asarray(cx), jnp.asarray(cx.T.copy()), jnp.asarray(table(NY)),
    )
    return tuple(o.reshape(slab, ZC, NY) for o in outs)


def solution(mesh):
    placed = (
        P("split", "dom", None),
        P("split", "dom", None),
        P("dom"),
        P("dom"),
        P("dom"),
        P("dom", None),
        P("dom", None),
    )
    return jax.shard_map(
        on_device,
        mesh=mesh,
        in_specs=placed,
        out_specs=(P("split", "dom", None),) * 3,
        check_vma=False,
    )
```

time: 290 us -> 83.2 us (0.29)
  blocking collectives: 143 us -> 0 us
  waiting for transfers between devices: 79.2 us -> 0 us
  Pallas kernels: 0 us -> 77 us
  starting transfers between devices: 32.1 us -> 0 us
  matrix products: 12.7 us -> 0 us
  other arithmetic: 10.2 us -> 0 us
  local copies, waits for them, and re-layouts: 8.67 us -> 3.46 us
    all_to_all x4 -> x0, blocking collectives: 105 us -> none  [the longest x1 77 us: neighbours(): lax.all_to_all(outgoing, 'dom', split_axis=0, concat_axis=0, tiled=True)]
    all_to_all x4 -> x0, waiting for transfers between devices: 79.2 us -> none  [the longest x1 62.4 us: neighbours(): lax.all_to_all(outgoing, 'dom', split_axis=0, concat_axis=0, tiled=True)]
    pallas_call x0 -> x1, Pallas kernels: none -> 77 us  [on_device(): pl.pallas_call(kernel, out_shape=(flat,) * 3, in_specs=[smem] * 5 + [vmem...]
    all_gather x2 -> x0, blocking collectives: 38.5 us -> none  [sent_together(): out, at, done = (lax.all_gather(both, axis, axis=dim, tiled=True), 0, [])]
    all_to_all x4 -> x0, starting transfers between devices: 32.1 us -> none  [the longest x1 14.2 us: neighbours(): lax.all_to_all(outgoing, 'dom', split_axis=0, concat_axis=0, tiled=True)]
    dot_general x16 -> x0, matrix products: 12.7 us -> none  [the longest x4 3.31 us: along_x(): jnp.dot(table, values, precision=HIGH, preferred_element_type=jnp.float32)]
    gather x12 -> x0, local copies, waits for them, and re-layouts: 5.63 us -> none  [the longest x8 3.33 us: shifted(): picked = jnp.take(picked, jnp.clip(cols, 0, width - 1), axis=2)]
    and x6 -> x0, other arithmetic: 5.23 us -> none  [the longest x2 1.31 us: shifted(): picked = jnp.take(picked, jnp.clip(cols, 0, width - 1), axis=2)]
  transfers between devices with their start and end apart: 4 -> 0, of which waited for: 4 -> 0; matrix products, arithmetic and copies ran while one was open for 3% -> 0% of each run, Pallas kernels for 0% -> 0%
where the time goes in v1:
time: 83.2 us; the launch traced here: 83 us
  Pallas kernels  77 us (93%)
  local copies, waits for them, and re-layouts  3.46 us (4%)
  between operations  2.59 us (3%)
    pallas_call x1, Pallas kernels, on_device(): pl.pallas_call(kernel, out_shape=(flat,) * 3, in_specs=[smem] * 5 + [vmem...  77 us
    unnamed x7, local copies, waits for them, and re-layouts  3.46 us

profile of v1, /device:TPU:1, one launch (start us, length us, event | category | flops | bytes accessed | tf_op | source)
XLA Modules:
  0.0 83.0 jit_solution(5044086393533164028)
XLA Ops:
  2.6 77.0 %shard_map.121 = (f32[512,128]{1,0:T(8,128)}, f32[512,128]{1,0:T(8,128)}, f32[512,128]{1,0:T(8,128)}) custom-call(s32[1]{0:T(128)S(6)} %copy.16.ext, s32[1]{0:T(128)S(6)} %copy.17.low, s32[1]{0:T(128)S(6)} %copy.18.upp, s32[1,2]{1,0:T(1,128)} %xs.1, s32[1,2]{1,0:T(1,128)} %ys.1, f32[512,128]{1,0:T(8,128)} %bitcast.5, f32[512,128]{1,0:T(8,128)} %bitcast.6, ...), custom_call_target="tpu_custom_call" | custom-call | tf_op jit(solution)/shard_map/pallas_call | solution.py:327
  79.5 0.0 copy-start.1
  79.5 1.7 %copy.19 = f32[8,64,128]{2,1,0:T(8,128)} copy(f32[8,64,128]{2,1,0:T(8,128)} %bitcast.9) | data formatting | bytes 524288
  81.3 0.0 copy-done.1
  81.3 0.0 copy-start
  81.3 0.7 copy.20
  82.0 0.3 copy-done
  82.3 0.7 copy.21
Async XLA Ops:
  79.5 1.7 %copy-start.1 = (f32[512,128]{1,0:T(8,128)S(1)}, f32[512,128]{1,0:T(8,128)}, u32[]{:S(2)}) copy-start(f32[512,128]{1,0:T(8,128)} %get-tuple-element.7) | copy-start | bytes 786436
  81.3 1.0 %copy-start = (f32[512,128]{1,0:T(8,128)S(1)}, f32[512,128]{1,0:T(8,128)}, u32[]{:S(2)}) copy-start(f32[512,128]{1,0:T(8,128)} %get-tuple-element.8) | copy-start | bytes 786436

commit v2 on v1

v2 whole, which is shorter than its diff:
```python
import math

import jax
import jax.numpy as jnp
import numpy as np
from jax import lax
from jax.experimental import pallas as pl
from jax.experimental.pallas import tpu as pltpu
from jax.sharding import PartitionSpec as P

F32 = jnp.float32
HIGH = lax.Precision.HIGH
XN, ZN, SN = 4, 16, 8
NX, NY, ZC = 64, 128, 64
QUARTER = 0.25
ST1, ST2, ST3 = 270.0 / 180.0, -27.0 / 180.0, 2.0 / 180.0
GAIN = [2.0 * (-1.0) ** n / math.factorial(2 * n + 2) for n in range(12)]
HALF_PI_2 = (math.pi / 2) ** 2
PAIRS = [(a, b) for a in range(6) for b in range(a, 6)]
MESH = pl.DeviceIdType.MESH


def dot(a, b):
    return jnp.dot(a, b, precision=HIGH, preferred_element_type=F32)


def dot_nt(a, b):
    return lax.dot_general(a, b, (((1,), (1,)), ((), ())), precision=HIGH, preferred_element_type=F32)


def gain_of(u):
    g = jnp.full(u.shape, GAIN[-1], F32)
    for c in GAIN[-2::-1]:
        g = g * u + c
    return g


def cos_table(k, x, length):
    n = k * (2.0 * x + 1.0)
    period = 4.0 * length
    rest = n - period * jnp.floor(n / period + 0.5)
    w = (math.pi / 2) * (rest / length)
    u = w * w
    scale = jnp.where(k == 0, jnp.sqrt(1.0 / length), jnp.sqrt(2.0 / length))
    return scale * (1.0 - 0.5 * u * gain_of(u))


def iota(shape, dim):
    return lax.broadcasted_iota(jnp.int32, shape, dim).astype(F32)


def low_rows(q1, q2, q3):
    return [ST1 * q1 + ST2 * q2 + ST3 * q3, ST2 * q1 + ST3 * q2, ST3 * q1]


def rows(i, n=ZC):
    return pl.ds(pl.multiple_of(i * n, n), n)


NEAR = sorted([(i, d) for i in range(XN) for d in range(-2, 3)], key=lambda p: min(p[0], XN - p[0]) + abs(p[1]))


def kernel(
    ext, low, upp, xs_, ys_, m0_, m1_, cx_, cxt_, cy_,
    nxt, cur, out, ztt,
    xs, ys, m0, m1, cx, cxt, cy,
    rt, rtt, w2, rtb, mz, b1, gn, h0, base2, sscr, kscr, kt, sb, st, nb, near, sel, far, ab, xab, yab, g, hs, hb, e1, ge, yo, yr,
    in_s, nb_s, nb_r, near_s, near_r, far_s, far_r, ab_s, ab_r, h_s, h_r, y_s, y_r,
):
    dom, me = lax.axis_index("dom"), lax.axis_index("split")
    px, pz = dom // ZN, lax.rem(dom, ZN)

    loads = [
        pltpu.make_async_copy(a, b, in_s.at[n])
        for n, (a, b) in enumerate(
            [(m0_, m0), (xs_, xs), (ys_, ys), (cx_, cx), (cy_, cy), (m1_, m1), (cxt_, cxt)]
        )
    ]
    for c in loads:
        c.start()

    def at(dx, dz):
        return lax.rem(px + dx + XN, XN) * ZN + lax.rem(pz + dz + ZN, ZN)

    def other(t):
        return lax.rem(me + t, SN)

    barrier = pltpu.get_barrier_semaphore()

    def greet(d, s):
        pl.semaphore_signal(barrier, inc=1, device_id=(d, s), device_id_type=MESH)

    for k in (2, 1, 3):
        greet(at(0, 4 * k), me)
    for i, d in NEAR[:0:-1]:
        greet(at(i, d), me)
    for t in range(1, SN):
        greet(dom, other(t))

    started = []

    def send(src, dst, ss, rs, d, s):
        c = pltpu.make_async_remote_copy(
            src_ref=src, dst_ref=dst, send_sem=ss, recv_sem=rs, device_id=(d, s), device_id_type=MESH
        )
        c.start()
        started.append(c)

    def arrived(dst, ss, rs):
        pltpu.make_async_remote_copy(
            src_ref=dst, dst_ref=dst, send_sem=ss, recv_sem=rs, device_id=(dom, me), device_id_type=MESH
        ).wait_recv()

    length = ext[0].astype(F32)

    def row_of(r):
        return jnp.where(r < 3, r, r + (length - 6.0))

    k8, r8 = iota((8, ZC), 1), iota((8, ZC), 0)
    rtt[...] = jnp.where((k8 < length) & (r8 < 6), cos_table(k8, row_of(r8), jnp.full((8, ZC), length)), 0.0)
    loads[0].wait()
    for i in range(8):
        sscr[i * 8 : i * 8 + 8, :] = dot(rtt[...], m0[i * ZC : (i + 1) * ZC, :])
    for r in range(6):
        st[0, r] = sscr[pl.ds(r, 8, stride=8), :]
    lowf, uppf = low[0].astype(F32), upp[0].astype(F32)
    nb[0, 0] = jnp.full((8, 128), lowf)
    nb[0, 1] = jnp.full((8, 128), uppf)
    pl.semaphore_wait(barrier, len(NEAR) - 1 + 3 + SN - 1)

    def half(d):
        return slice(3, 6) if d == 2 else slice(0, 3) if d == -2 else slice(0, 6)

    def send_near(step):
        for n in range(len(NEAR) - 1, 0, -1):
            i, d = NEAR[n]
            h = half(d)
            send(st.at[step, h], near.at[step, n, h], near_s.at[step, n], near_r.at[step, n], at(i, d), me)

    send_near(0)
    for k in range(1, 4):
        send(nb.at[0], nb.at[k], nb_s.at[k], nb_r.at[k], at(0, -4 * k), me)

    for c in loads[1:5]:
        c.wait()

    for f in range(2):
        for c, n, move, is_x in ((cy, NY, ys[0, f], False), (cx, NX, xs[0, f], True)):
            move = move.astype(F32)
            row, col = iota((n, n), 0), iota((n, n), 1)
            put = (col == row + move).astype(F32)
            tab = c[...]
            seen = ((col + move >= 0) & (col + move < n)).astype(F32)
            moved = dot(tab, put)
            b = dot_nt(tab * seen, tab)
            if is_x:
                has = jnp.where(jnp.full((n, n), uppf if f else lowf) >= 0, QUARTER, 0.0)
                xab[f, :, 0:NX] = dot_nt(moved, tab) * has
                xab[f, :, NX : 2 * NX] = -b * has
            else:
                yab[f, 0] = dot_nt(tab, moved)
                yab[f, 1] = b

    def put_ab(step, w, lo, up):
        ab[step, w, me, 0:3] = dot(jnp.concatenate(lo, axis=0), yab[0, w]).reshape(3, 8, NY)
        ab[step, w, me, 3:6] = dot(jnp.concatenate(up, axis=0), yab[1, w]).reshape(3, 8, NY)
        for t in range(1, SN):
            send(ab.at[step, w, me], ab.at[step, w, me], ab_s.at[step, w, t], ab_r.at[step, w, t], dom, other(t))

    def own_part(step):
        p = [st[step, r] for r in range(6)]
        put_ab(step, 1, low_rows(p[0], p[1], p[2]), low_rows(p[5], p[4], p[3])[::-1])

    def to_far(step):
        lo = [[jnp.zeros((8, NY), F32)] * 3 for _ in range(4)]
        up = [[jnp.zeros((8, NY), F32)] * 3 for _ in range(4)]
        for n, (i, d) in enumerate(NEAR):
            if n == 0:
                block = st.at[step]
            else:
                h = half(d)
                arrived(near.at[step, n, h], near_s.at[step, n], near_r.at[step, n])
                block = near.at[step, n]
            who = at(-i, -d).astype(F32)
            if d >= -1:
                b = [block[r] for r in range(3, 6)]
                for k in range(4):
                    hit = nb[k, 0] == who
                    lo[k] = [jnp.where(hit, v, a) for v, a in zip(b, lo[k])]
            if d <= 1:
                b = [block[r] for r in range(3)]
                for k in range(4):
                    hit = nb[k, 1] == who
                    up[k] = [jnp.where(hit, v, a) for v, a in zip(b, up[k])]
        for k in (2, 1, 3, 0):
            for r in range(3):
                sel[step, k, r] = lo[k][r]
                sel[step, k, r + 3] = up[k][r]
            if k:
                send(sel.at[step, k], far.at[step, k], far_s.at[step, k], far_r.at[step, k], at(0, 4 * k), me)

    def from_far(step):
        q = [sel[step, 0, r] for r in range(6)]
        for k in (1, 3, 2):
            arrived(far.at[step, k], far_s.at[step, k], far_r.at[step, k])
            q = [a + far[step, k, r] for r, a in enumerate(q)]
        put_ab(step, 0, low_rows(q[2], q[1], q[0]), low_rows(q[3], q[4], q[5])[::-1])

    def gathered(step):
        for w in (1, 0):
            for t in range(1, SN):
                arrived(ab.at[step, w, other(SN - t)], ab_s.at[step, w, t], ab_r.at[step, w, t])

    def sources(step, r):
        return jnp.concatenate([ab[step, w, :, r].reshape(NX, NY) for w in range(2)], axis=0)

    def whole(step):
        for r in range(6):
            g[step, r * NX : (r + 1) * NX, :] = dot(xab[r // 3], sources(step, r))
        g[step, 6 * NX :, :] = jnp.zeros((2 * NX, NY), F32)

    def forced(step, i):
        return gn[rows(i), :] * dot(rt[...], g[step, pl.ds(me * 8 + i, 8, stride=NX), :])

    own_part(0)

    kz = iota((ZC, NY), 0)
    live = kz < length
    lv = jnp.full((ZC, NY), length)
    flat = kz / lv
    flat = flat * flat + (iota((ZC, NY), 1) / NY) ** 2

    def twice(i):
        kx = (me * 8 + i).astype(F32) / NX
        return HALF_PI_2 * (flat + kx * kx)

    loads[5].wait()

    def bases(i, _):
        u = twice(i)
        gain = gain_of(u)
        tw = 2.0 - u * gain
        m = jnp.where(live, m0[rows(i), :], 0.0)
        base = tw * m - jnp.where(live, m1[rows(i), :], 0.0)
        mz[rows(i), :] = m
        gn[rows(i), :] = gain
        b1[rows(i), :] = base
        h0[rows(i), :] = tw * base - m
        return 0

    lax.fori_loop(0, 8, bases, 0)
    for k in range(1, 4):
        arrived(nb.at[k], nb_s.at[k], nb_r.at[k])
    to_far(0)

    for n, (a, b) in enumerate(PAIRS):
        w2[n : n + 1, :] = rtt[a : a + 1, :] * rtt[b : b + 1, :]
    w2[21:24, :] = jnp.zeros((3, ZC), F32)

    def strips(i, _):
        sscr[rows(i, 8), :] = dot(rtt[...], b1[rows(i), :])
        kscr[rows(i, 24), :] = dot(w2[...], gn[rows(i), :])
        return 0

    lax.fori_loop(0, 8, strips, 0)
    for r in range(6):
        sb[r] = sscr[pl.ds(r, 8, stride=8), :]
    for n in range(21):
        kt[n] = kscr[pl.ds(n, 8, stride=24), :]

    def turn(k, _):
        hs[k] = h0[pl.ds(k, 8, stride=ZC), :]
        return 0

    lax.fori_loop(0, ZC, turn, 0, unroll=8)
    for t in range(1, SN):
        dst = pl.multiple_of(other(t) * 8, 8)
        send(hs.at[pl.ds(dst, 8)], hb.at[me], h_s.at[t], h_r.at[t], dom, other(t))
    hb[me] = hs[rows(me, 8)]
    from_far(0)

    k8, r8 = iota((ZC, 8), 0), iota((ZC, 8), 1)
    rt[...] = jnp.where((k8 < length) & (r8 < 6), cos_table(k8, row_of(r8), jnp.full((ZC, 8), length)), 0.0)
    kk, zz = iota((ZC, ZC), 1), iota((ZC, ZC), 0)
    ztt[...] = jnp.where((kk < length) & (zz < length), cos_table(kk, zz, jnp.full((ZC, ZC), length)), 0.0)
    for j in range(8):
        c = rt[pl.ds(me * 8 + j, 1), :]
        for r in range(6):
            rtb[j * 8 + r : j * 8 + r + 1, :] = jnp.broadcast_to(c[:, r : r + 1], (1, NY))
    gathered(0)

    mine = [xab[f, rows(me, 8), :] for f in range(2)]
    g1 = [dot(mine[r // 3], sources(0, r)) for r in range(6)]
    for r in range(6):
        s = sb[r]
        for q in range(6):
            s = s + kt[PAIRS.index((min(r, q), max(r, q)))] * g1[q]
        st[1, r] = s
    send_near(1)
    own_part(1)
    whole(0)

    for t in range(1, SN):
        arrived(hb.at[other(SN - t)], h_s.at[t], h_r.at[t])
    kx2 = (iota((NX, NY), 0) / NX) ** 2 + (iota((NX, NY), 1) / NY) ** 2

    def rowsum(step, j):
        total = rtb[pl.ds(j * 8, 1), :] * g[step, 0:NX, :]
        for r in range(1, 6):
            total = total + rtb[pl.ds(j * 8 + r, 1), :] * g[step, r * NX : (r + 1) * NX, :]
        return total

    def early(j, _):
        z = jnp.full((NX, NY), (me * 8 + j).astype(F32)) / lv
        u = HALF_PI_2 * (kx2 + z * z)
        gain = gain_of(u)
        ge[j] = gain
        e1[j] = hb[:, j].reshape(NX, NY) + gain * (2.0 - u * gain) * rowsum(0, j)
        return 0

    lax.fori_loop(0, 8, early, 0)
    to_far(1)

    def step_one(i, _):
        m = b1[rows(i), :] + forced(0, i)
        cur[rows(i), :] = m
        base2[rows(i), :] = (2.0 - twice(i) * gn[rows(i), :]) * m - mz[rows(i), :]
        return 0

    lax.fori_loop(0, 8, step_one, 0)
    loads[6].wait()
    from_far(1)
    gathered(1)
    whole(1)

    for half_j in range(2):
        js = range(half_j * 4, half_j * 4 + 4)
        e = jnp.concatenate([e1[j] + ge[j] * rowsum(1, j) for j in js], axis=1)
        x = dot(cxt[...], e)
        for n, j in enumerate(js):
            yo[half_j, :, n] = x[:, n * NY : (n + 1) * NY].reshape(SN, 8, NY)
        for t in range(1, SN):
            send(yo.at[half_j, other(t)], yr.at[me, rows(half_j, 4)], y_s.at[half_j, t], y_r.at[half_j, t], dom, other(t))

    def step_two(i, _):
        nxt[rows(i), :] = base2[rows(i), :] + forced(1, i)
        return 0

    lax.fori_loop(0, 8, step_two, 0)
    out[me, 0:4] = yo[0, me]
    out[me, 4:8] = yo[1, me]
    for half_j in range(2):
        for t in range(1, SN):
            src = other(SN - t)
            part = rows(half_j, 4)
            arrived(yr.at[src, part], y_s.at[half_j, t], y_r.at[half_j, t])
            out[src, half_j * 4 : half_j * 4 + 4] = yr[src, half_j * 4 : half_j * 4 + 4]

    for c in started:
        c.wait_send()


def finish(nxt_, cur_, y, ztt, cy, nxt, cur, prs, p, sems):
    copies = [pltpu.make_async_copy(nxt_, nxt, sems.at[0]), pltpu.make_async_copy(cur_, cur, sems.at[1])]
    for c in copies:
        c.start()
    for h in range(2):
        a = dot(ztt[...], jnp.concatenate([y[:, :, i].reshape(ZC, NY) for i in range(h * 4, h * 4 + 4)], axis=1))
        a = jnp.concatenate([a[:, n * NY : (n + 1) * NY] for n in range(4)], axis=0)
        p[h * 4 * ZC : (h + 1) * 4 * ZC, :] = dot(a, cy[...])
        c = pltpu.make_async_copy(p.at[rows(h, 4 * ZC)], prs.at[rows(h, 4 * ZC)], sems.at[2 + h])
        c.start()
        copies.append(c)
    for c in copies:
        c.wait()


def table(n):
    k, x = np.arange(n)[:, None], np.arange(n)[None, :]
    return (np.where(k == 0, math.sqrt(1 / n), math.sqrt(2 / n)) * np.cos(math.pi * k * (x + 0.5) / n)).astype(np.float32)


def on_device(modes_now, modes_prev, z_extent, lower_nbr, upper_nbr, x_shift, y_shift):
    slab = modes_now.shape[0]
    flat = jax.ShapeDtypeStruct((slab * ZC, NY), F32)
    cx, cy = table(NX), jnp.asarray(table(NY))
    hbm, vmem = pl.BlockSpec(memory_space=pltpu.HBM), pl.BlockSpec(memory_space=pltpu.VMEM)
    v = lambda *s: pltpu.VMEM(s, F32)
    sm = lambda *s: pltpu.SMEM(s, jnp.int32)
    dma = pltpu.SemaphoreType.DMA
    nxt, cur, y, ztt = pl.pallas_call(
        kernel,
        out_shape=(flat, flat, jax.ShapeDtypeStruct((8, 8, 8, NY), F32), jax.ShapeDtypeStruct((ZC, ZC), F32)),
        in_specs=[pl.BlockSpec(memory_space=pltpu.SMEM)] * 3 + [hbm] * 7,
        out_specs=(vmem,) * 4,
        scratch_shapes=[
            sm(1, 2), sm(1, 2), v(512, NY), v(512, NY), v(NX, NX), v(NX, NX), v(NY, NY),
            v(ZC, 8), v(8, ZC), v(24, ZC), v(64, NY), v(512, NY), v(512, NY), v(512, NY), v(512, NY), v(512, NY),
            v(64, NY), v(192, NY), v(21, 8, NY), v(6, 8, NY),
            v(2, 6, 8, NY), v(4, 2, 8, NY), v(2, 20, 6, 8, NY), v(2, 4, 6, 8, NY), v(2, 4, 6, 8, NY),
            v(2, 2, 8, 6, 8, NY), v(2, NX, 2 * NX), v(2, 2, NY, NY), v(2, 8 * NX, NY),
            v(ZC, 8, NY), v(8, 8, 8, NY), v(8, NX, NY), v(8, NX, NY), v(2, 8, 4, 8, NY), v(8, 8, 8, NY),
            dma((7,)), dma((4,)), dma((4,)), dma((2, 20)), dma((2, 20)), dma((2, 4)), dma((2, 4)),
            dma((2, 2, 8)), dma((2, 2, 8)), dma((8,)), dma((8,)), dma((2, 8)), dma((2, 8)),
        ],
        compiler_params=pltpu.CompilerParams(collective_id=0, has_side_effects=True, vmem_limit_bytes=20 * 2**20),
    )(z_extent, lower_nbr, upper_nbr, *[
        pltpu.with_memory_space_constraint(a, pltpu.HBM)
        for a in (
            x_shift, y_shift,
            modes_now.reshape(slab * ZC, NY), modes_prev.reshape(slab * ZC, NY),
            jnp.asarray(cx), jnp.asarray(cx.T.copy()), cy,
        )
    ])
    anyw = pl.BlockSpec(memory_space=pl.ANY)
    outs = pl.pallas_call(
        finish,
        out_shape=(flat,) * 3,
        in_specs=[anyw, anyw, vmem, vmem, vmem],
        out_specs=(hbm,) * 3,
        scratch_shapes=[v(512, NY), dma((4,))],
        compiler_params=pltpu.CompilerParams(vmem_limit_bytes=8 * 2**20),
    )(nxt, cur, y, ztt, cy)
    return tuple(o.reshape(slab, ZC, NY) for o in outs)


def solution(mesh):
    placed = (
        P("split", "dom", None),
        P("split", "dom", None),
        P("dom"),
        P("dom"),
        P("dom"),
        P("dom", None),
        P("dom", None),
    )
    return jax.shard_map(
        on_device,
        mesh=mesh,
        in_specs=placed,
        out_specs=(P("split", "dom", None),) * 3,
        check_vma=False,
    )
```

time: 83.2 us -> 72 us (0.87)
  Pallas kernels: 77 us -> 69.2 us
  local copies, waits for them, and re-layouts: 3.46 us -> 0.01 us
    pallas_call x1 -> x2, Pallas kernels: 77 us -> 69.2 us  [the longest x1 67.9 us: on_device(): pl.pallas_call(kernel, out_shape=(flat, flat, jax.ShapeDtypeStruct((8, 8,...]
    unnamed x7 -> x2, local copies, waits for them, and re-layouts: 3.46 us -> 0.01 us
where the time goes in v2:
time: 72 us; the launch traced here: 71.8 us
  Pallas kernels  69.2 us (96%)
  between operations  2.59 us (4%)
    pallas_call x1, Pallas kernels, on_device(): pl.pallas_call(kernel, out_shape=(flat, flat, jax.ShapeDtypeStruct((8, 8,...  67.9 us

profile of v2, /device:TPU:1, one launch (start us, length us, event | category | flops | bytes accessed | tf_op | source)
XLA Modules:
  0.0 71.8 jit_solution(4063360799289376469)
XLA Ops:
  2.6 0.0 copy-start
  2.6 67.9 %shard_map.121 = (f32[512,128]{1,0:T(8,128)S(1)}, f32[512,128]{1,0:T(8,128)S(1)}, f32[8,8,8,128]{3,2,1,0:T(8,128)S(1)}, f32[64,64]{1,0:T(8,128)S(1)}) custom-call(s32[1]{0:T(128)S(6)} %copy.13.ext, s32[1]{0:T(128)S(6)} %copy.14.low, s32[1]{0:T(128)S(6)} %copy.15.upp, s32[1,2]{1,0:T(1,128)} %xs_.1, s32[1,2]{1,0:T(1,128)} %ys_.1, f32[512,128]{1,0:T(8,128)} %bitcast.5, ...), custom_call_target="tpu_custom_call" | custom-call | tf_op jit(solution)/shard_map/pallas_call | solution.py:391
  70.4 0.0 copy-done
  70.5 1.4 %shard_map.122 = (f32[512,128]{1,0:T(8,128)}, f32[512,128]{1,0:T(8,128)}, f32[512,128]{1,0:T(8,128)}) custom-call(f32[512,128]{1,0:T(8,128)S(1)} %get-tuple-element.10.nxt_, f32[512,128]{1,0:T(8,128)S(1)} %get-tuple-element.11.cur_, f32[8,8,8,128]{3,2,1,0:T(8,128)S(1)} %get-tuple-element.12.y, f32[64,64]{1,0:T(8,128)S(1)} %get-tuple-element.13.ztt, ...), custom_call_target="tpu_custom_call" | custom-call | tf_op jit(solution)/shard_map/pallas_call | solution.py:416
Async XLA Ops:
  2.6 67.9 %copy-start = (f32[128,128]{1,0:T(8,128)S(1)}, f32[128,128]{1,0:T(8,128)}, u32[]{:S(2)}) copy-start(f32[128,128]{1,0:T(8,128)} %constant.6.clone.cy_.cy) | copy-start | bytes 196612

commit v3 on v2

v3 whole, which is shorter than its diff:
```python
import math

import jax
import jax.numpy as jnp
import numpy as np
from jax import lax
from jax.experimental import pallas as pl
from jax.experimental.pallas import tpu as pltpu
from jax.sharding import PartitionSpec as P

F32 = jnp.float32
HIGH = lax.Precision.HIGH
XN, ZN, SN = 4, 16, 8
NX, NY, ZC = 64, 128, 64
QUARTER = 0.25
ST1, ST2, ST3 = 270.0 / 180.0, -27.0 / 180.0, 2.0 / 180.0
GAIN = [2.0 * (-1.0) ** n / math.factorial(2 * n + 2) for n in range(12)]
HALF_PI_2 = (math.pi / 2) ** 2
PAIRS = [(a, b) for a in range(6) for b in range(a, 6)]
MESH = pl.DeviceIdType.MESH


def dot(a, b):
    return jnp.dot(a, b, precision=HIGH, preferred_element_type=F32)


def dot_nt(a, b):
    return lax.dot_general(a, b, (((1,), (1,)), ((), ())), precision=HIGH, preferred_element_type=F32)


def gain_of(u):
    g = jnp.full(u.shape, GAIN[-1], F32)
    for c in GAIN[-2::-1]:
        g = g * u + c
    return g


def cos_table(k, x, length):
    n = k * (2.0 * x + 1.0)
    period = 4.0 * length
    rest = n - period * jnp.floor(n / period + 0.5)
    w = (math.pi / 2) * (rest / length)
    u = w * w
    scale = jnp.where(k == 0, jnp.sqrt(1.0 / length), jnp.sqrt(2.0 / length))
    return scale * (1.0 - 0.5 * u * gain_of(u))


def iota(shape, dim):
    return lax.broadcasted_iota(jnp.int32, shape, dim).astype(F32)


def low_rows(q1, q2, q3):
    return [ST1 * q1 + ST2 * q2 + ST3 * q3, ST2 * q1 + ST3 * q2, ST3 * q1]


def rows(i, n=ZC):
    return pl.ds(pl.multiple_of(i * n, n), n)


WINDOWS = [
    sorted([(i, d) for i in range(XN) for d in ds], key=lambda p: min(p[0], XN - p[0]) + abs(p[1]))
    for ds in (range(-1, 3), range(-2, 2))
]
GREET = [(i, d) for d in (-2, 2, -1, 1, 0) for i in (2, 1, 3, 0) if (i, d) != (0, 0)]
KH = ZC // 2


def kernel(
    ext, low, upp, xs_, ys_, m0_, m1_, cx_, cxt_, cy_,
    nxt, cur, out, ztt,
    xs, ys, m0, m1, cx, cxt, cy,
    rt, rtt, w2, rtb, mz, b1, gn, h0, base2, sscr, kscr, kt, sb, st, nb, near, sel, far, aa, bb, xa, xb, yab, gb, g,
    hs, hb, e1, ge, yo, yr,
    in_s, nb_s, nb_r, near_s, near_r, far_s, far_r, aa_s, aa_r, bb_s, bb_r, h_s, h_r, y_s, y_r,
):
    dom, me = lax.axis_index("dom"), lax.axis_index("split")
    px, pz = dom // ZN, lax.rem(dom, ZN)
    chip, core = me // 2, lax.rem(me, 2)

    loads = [
        pltpu.make_async_copy(a, b, in_s.at[n])
        for n, (a, b) in enumerate([(m0_, m0), (xs_, xs), (ys_, ys), (cx_, cx), (cy_, cy), (m1_, m1), (cxt_, cxt)])
    ]
    for c in loads:
        c.start()

    def at(dx, dz):
        return lax.rem(px + dx + XN, XN) * ZN + lax.rem(pz + dz + ZN, ZN)

    def other(t):
        return lax.rem(me + t, SN)

    barrier = pltpu.get_barrier_semaphore()

    def greet(d, s):
        pl.semaphore_signal(barrier, inc=1, device_id=(d, s), device_id_type=MESH)

    for k in (2, 1, 3):
        greet(at(0, 4 * k), me)
    for i, d in GREET:
        greet(at(i, d), me)
    for t in range(1, SN):
        greet(dom, other(t))

    started = []

    def send(src, dst, ss, rs, d, s):
        c = pltpu.make_async_remote_copy(
            src_ref=src, dst_ref=dst, send_sem=ss, recv_sem=rs, device_id=(d, s), device_id_type=MESH
        )
        c.start()
        started.append(c)

    def arrived(dst, ss, rs):
        pltpu.make_async_remote_copy(
            src_ref=dst, dst_ref=dst, send_sem=ss, recv_sem=rs, device_id=(dom, me), device_id_type=MESH
        ).wait_recv()

    length = ext[0].astype(F32)

    def row_of(r):
        return jnp.where(r < 3, r, r + (length - 6.0))

    def row_table(k, r):
        return jnp.where((k < length) & (r < 6), cos_table(k, row_of(r), jnp.full(k.shape, length)), 0.0)

    rtt[...] = row_table(iota((8, ZC), 1), iota((8, ZC), 0))
    lowf, uppf = low[0].astype(F32), upp[0].astype(F32)
    nb[0, 0] = jnp.full((8, 128), lowf)
    nb[0, 1] = jnp.full((8, 128), uppf)
    loads[0].wait()
    for i in range(8):
        sscr[i * 8 : i * 8 + 8, :] = dot(rtt[...], m0[i * ZC : (i + 1) * ZC, :])
    for r in range(6):
        st[0, r] = sscr[pl.ds(r, 8, stride=8), :]
    pl.semaphore_wait(barrier, len(GREET) + 3 + SN - 1)

    def strip_rows(f):
        return slice(3, 6) if f == 0 else slice(0, 3)

    def send_near(step):
        for f in range(2):
            for n in range(15, 0, -1):
                i, d = WINDOWS[f][n]
                send(
                    st.at[step, strip_rows(f)], near.at[step, f, n],
                    near_s.at[step, f, n], near_r.at[step, f, n], at(i, d), me,
                )

    for k in (2, 1, 3):
        send(nb.at[0], nb.at[k], nb_s.at[k], nb_r.at[k], at(0, -4 * k), me)
    send_near(0)

    for c in loads[1:5]:
        c.wait()

    for f in range(2):
        for c, n, move, is_x in ((cy, NY, ys[0, f], False), (cx, NX, xs[0, f], True)):
            move = move.astype(F32)
            row, col = iota((n, n), 0), iota((n, n), 1)
            put = (col == row + move).astype(F32)
            tab = c[...]
            seen = ((col + move >= 0) & (col + move < n)).astype(F32)
            moved = dot(tab, put)
            b = dot_nt(tab * seen, tab)
            if is_x:
                has = jnp.where(jnp.full((n, n), uppf if f else lowf) >= 0, QUARTER, 0.0)
                xa[f] = dot_nt(moved, tab) * has
                xb[f] = -b * has
            else:
                yab[f, 0] = dot_nt(tab, moved)
                yab[f, 1] = b

    def own_part(step):
        p = [st[step, r] for r in range(6)]
        for f, part in enumerate((low_rows(p[0], p[1], p[2]), low_rows(p[5], p[4], p[3])[::-1])):
            bb[step, me, 3 * f : 3 * f + 3] = dot(jnp.concatenate(part, axis=0), yab[f, 1]).reshape(3, 8, NY)
        for t in range(1, SN):
            send(bb.at[step, me], bb.at[step, me], bb_s.at[step, t], bb_r.at[step, t], dom, other(t))

    def to_far(step, f):
        acc = [[jnp.zeros((8, NY), F32)] * 3 for _ in range(4)]
        rows_f = strip_rows(f)
        for n, (i, d) in enumerate(WINDOWS[f]):
            if n == 0:
                block = [st[step, r] for r in range(rows_f.start, rows_f.stop)]
            else:
                arrived(near.at[step, f, n], near_s.at[step, f, n], near_r.at[step, f, n])
                block = [near[step, f, n, r] for r in range(3)]
            who = at(-i, -d).astype(F32)
            for k in range(4):
                hit = nb[k, f] == who
                acc[k] = [jnp.where(hit, v, a) for v, a in zip(block, acc[k])]
        for k in (2, 1, 3, 0):
            for r in range(3):
                sel[step, f, k, r] = acc[k][r]
            if k:
                send(
                    sel.at[step, f, k], far.at[step, f, k],
                    far_s.at[step, f, k], far_r.at[step, f, k], at(0, 4 * k), me,
                )

    def from_far(step, f):
        q = [sel[step, f, 0, r] for r in range(3)]
        for k in (1, 3, 2):
            arrived(far.at[step, f, k], far_s.at[step, f, k], far_r.at[step, f, k])
            q = [a + far[step, f, k, r] for r, a in enumerate(q)]
        part = low_rows(*q)[::-1] if f else low_rows(*q[::-1])
        aa[step, f, me] = dot(jnp.concatenate(part, axis=0), yab[f, 0]).reshape(3, 8, NY)
        for t in range(1, SN):
            send(aa.at[step, f, me], aa.at[step, f, me], aa_s.at[step, f, t], aa_r.at[step, f, t], dom, other(t))

    def gathered_own(step):
        for t in range(1, SN):
            arrived(bb.at[step, other(SN - t)], bb_s.at[step, t], bb_r.at[step, t])

    def gathered(step, f):
        for t in range(1, SN):
            arrived(aa.at[step, f, other(SN - t)], aa_s.at[step, f, t], aa_r.at[step, f, t])

    def theirs(step, r):
        return aa[step, r // 3, :, r % 3].reshape(NX, NY)

    def ours(step, r):
        return bb[step, :, r].reshape(NX, NY)

    def forced(step, i):
        return gn[rows(i), :] * dot(rt[...], g[step, pl.ds(me * 8 + i, 8, stride=NX), :])

    own_part(0)

    kz = iota((ZC, NY), 0)
    live = kz < length
    lv = jnp.full((ZC, NY), length)
    flat = kz / lv
    flat = flat * flat + (iota((ZC, NY), 1) / NY) ** 2

    def twice(i):
        kx = (me * 8 + i).astype(F32) / NX
        return HALF_PI_2 * (flat + kx * kx)

    loads[5].wait()

    def bases(i, _):
        u = twice(i)
        gain = gain_of(u)
        tw = 2.0 - u * gain
        m = jnp.where(live, m0[rows(i), :], 0.0)
        base = tw * m - jnp.where(live, m1[rows(i), :], 0.0)
        mz[rows(i), :] = m
        gn[rows(i), :] = gain
        b1[rows(i), :] = base
        h0[rows(i), :] = tw * base - m
        return 0

    lax.fori_loop(0, 8, bases, 0)
    for k in (1, 3, 2):
        arrived(nb.at[k], nb_s.at[k], nb_r.at[k])
    to_far(0, 0)
    to_far(0, 1)

    def turn(k, _):
        hs[k] = h0[pl.ds(k, 8, stride=ZC), :]
        return 0

    lax.fori_loop(0, ZC, turn, 0, unroll=8)

    def send_h(part):
        for t in range(1, SN):
            first = pl.multiple_of(lax.rem(other(t), 2) * KH + part * 16, 16)
            send(
                hs.at[pl.ds(first, 16)], hb.at[me, rows(part, 16)], h_s.at[part, t], h_r.at[part, t], dom, other(t)
            )

    send_h(0)
    hb[me] = hs[rows(core, KH)]
    for n, (a, b) in enumerate(PAIRS):
        w2[n : n + 1, :] = rtt[a : a + 1, :] * rtt[b : b + 1, :]
    w2[21:24, :] = jnp.zeros((3, ZC), F32)

    def strips(i, _):
        sscr[rows(i, 8), :] = dot(rtt[...], b1[rows(i), :])
        kscr[rows(i, 24), :] = dot(w2[...], gn[rows(i), :])
        return 0

    lax.fori_loop(0, 8, strips, 0)
    for r in range(6):
        sb[r] = sscr[pl.ds(r, 8, stride=8), :]
    for n in range(21):
        kt[n] = kscr[pl.ds(n, 8, stride=24), :]
    gathered_own(0)
    for r in range(6):
        gb[r] = dot(xb[r // 3, rows(me, 8), :], ours(0, r))
    from_far(0, 0)
    from_far(0, 1)

    rt[...] = row_table(iota((ZC, 8), 0), iota((ZC, 8), 1))
    kk, zz = iota((ZC, ZC), 1), iota((ZC, ZC), 0)
    ztt[...] = jnp.where((kk < length) & (zz < length), cos_table(kk, zz, jnp.full((ZC, ZC), length)), 0.0)
    g1 = []
    for f in range(2):
        gathered(0, f)
        for r in range(3 * f, 3 * f + 3):
            g1.append(gb[r] + dot(xa[f, rows(me, 8), :], theirs(0, r)))
    for r in range(6):
        s = sb[r]
        for q in range(6):
            s = s + kt[PAIRS.index((min(r, q), max(r, q)))] * g1[q]
        st[1, r] = s
    send_near(1)
    own_part(1)
    send_h(1)
    for step in range(2):
        g[step, 6 * NX :, :] = jnp.zeros((2 * NX, NY), F32)
    for r in range(6):
        g[0, r * NX : (r + 1) * NX, :] = dot(xb[r // 3], ours(0, r)) + dot(xa[r // 3], theirs(0, r))
    shape = (KH, 8, NY)
    rtb[...] = row_table(iota(shape, 0) + (core * KH).astype(F32), iota(shape, 1))

    kx2 = (iota((NX, NY), 0) / NX) ** 2 + (iota((NX, NY), 1) / NY) ** 2

    def early(j, _):
        z = jnp.full((NX, NY), (core * KH + j).astype(F32)) / lv
        u = HALF_PI_2 * (kx2 + z * z)
        gain = gain_of(u)
        total = rtb[j, 0:1, :] * g[0, 0:NX, :]
        for r in range(1, 6):
            total = total + rtb[j, r : r + 1, :] * g[0, r * NX : (r + 1) * NX, :]
        ge[j] = gain
        e1[j] = hb[:, j].reshape(NX, NY) + gain * (2.0 - u * gain) * total
        return 0

    def arrived_h(part):
        for t in range(1, SN):
            arrived(hb.at[other(SN - t), rows(part, 16)], h_s.at[part, t], h_r.at[part, t])

    arrived_h(0)
    lax.fori_loop(0, 16, early, 0)
    to_far(1, 0)
    to_far(1, 1)

    def step_one(i, _):
        m = b1[rows(i), :] + forced(0, i)
        cur[rows(i), :] = m
        base2[rows(i), :] = (2.0 - twice(i) * gn[rows(i), :]) * m - mz[rows(i), :]
        return 0

    gathered_own(1)
    for r in range(6):
        g[1, r * NX : (r + 1) * NX, :] = dot(xb[r // 3], ours(1, r))
    arrived_h(1)
    lax.fori_loop(16, KH, early, 0)
    loads[6].wait()
    from_far(1, 0)
    from_far(1, 1)
    lax.fori_loop(0, 8, step_one, 0)
    for f in range(2):
        gathered(1, f)
        for r in range(3 * f, 3 * f + 3):
            g[1, r * NX : (r + 1) * NX, :] += dot(xa[f], theirs(1, r))

    twin = 1 - core
    cx16 = cxt[rows(chip, 16), :]
    for part in range(4):
        parts = []
        for j in range(part * 8, part * 8 + 8, 2):
            weights = [[jnp.broadcast_to(rtb[jj, r : r + 1, :], (8, NY)) for r in range(6)] for jj in (j, j + 1)]
            tiles = [[], []]
            for x in range(8):
                src = [g[1, r * NX + x * 8 : r * NX + x * 8 + 8, :] for r in range(6)]
                for n in range(2):
                    total = weights[n][0] * src[0]
                    for r in range(1, 6):
                        total = total + weights[n][r] * src[r]
                    at_x = slice(x * 8, x * 8 + 8)
                    tiles[n].append(e1[j + n, at_x, :] + ge[j + n, at_x, :] * total)
            parts += [jnp.concatenate(t, axis=0) for t in tiles]
        x = dot(cx16, jnp.concatenate(parts, axis=1))
        for c in range(2):
            for j in range(8):
                yo[c, part * 8 + j] = x[c * 8 : c * 8 + 8, j * NY : (j + 1) * NY]
        p8 = rows(part, 8)
        send(yo.at[twin, p8], yr.at[p8], y_s.at[part], y_r.at[part], dom, chip * 2 + twin)

    def step_two(i, _):
        nxt[rows(i), :] = base2[rows(i), :] + forced(1, i)
        return 0

    lax.fori_loop(0, 8, step_two, 0)
    out[core] = yo[core]
    for part in range(4):
        p8 = rows(part, 8)
        arrived(yr.at[p8], y_s.at[part], y_r.at[part])
        out[twin, p8] = yr[p8]

    for c in started:
        c.wait_send()


def finish(nxt_, cur_, y, ztt, cy, nxt, cur, prs, p, sems):
    copies = [pltpu.make_async_copy(nxt_, nxt, sems.at[0]), pltpu.make_async_copy(cur_, cur, sems.at[1])]
    for c in copies:
        c.start()
    for h in range(2):
        a = dot(ztt[...], jnp.concatenate([y[:, :, i].reshape(ZC, NY) for i in range(h * 4, h * 4 + 4)], axis=1))
        a = jnp.concatenate([a[:, n * NY : (n + 1) * NY] for n in range(4)], axis=0)
        p[h * 4 * ZC : (h + 1) * 4 * ZC, :] = dot(a, cy[...])
        c = pltpu.make_async_copy(p.at[rows(h, 4 * ZC)], prs.at[rows(h, 4 * ZC)], sems.at[2 + h])
        c.start()
        copies.append(c)
    for c in copies:
        c.wait()


def table(n):
    k, x = np.arange(n)[:, None], np.arange(n)[None, :]
    return (np.where(k == 0, math.sqrt(1 / n), math.sqrt(2 / n)) * np.cos(math.pi * k * (x + 0.5) / n)).astype(np.float32)


def on_device(modes_now, modes_prev, z_extent, lower_nbr, upper_nbr, x_shift, y_shift):
    slab = modes_now.shape[0]
    flat = jax.ShapeDtypeStruct((slab * ZC, NY), F32)
    cx, cy = table(NX), jnp.asarray(table(NY))
    hbm, vmem = pl.BlockSpec(memory_space=pltpu.HBM), pl.BlockSpec(memory_space=pltpu.VMEM)
    v = lambda *s: pltpu.VMEM(s, F32)
    sm = lambda *s: pltpu.SMEM(s, jnp.int32)
    dma = pltpu.SemaphoreType.DMA
    nxt, cur, y, ztt = pl.pallas_call(
        kernel,
        out_shape=(flat, flat, jax.ShapeDtypeStruct((2, KH, 8, NY), F32), jax.ShapeDtypeStruct((ZC, ZC), F32)),
        in_specs=[pl.BlockSpec(memory_space=pltpu.SMEM)] * 3 + [hbm] * 7,
        out_specs=(vmem,) * 4,
        scratch_shapes=[
            sm(1, 2), sm(1, 2), v(512, NY), v(512, NY), v(NX, NX), v(NX, NX), v(NY, NY),
            v(ZC, 8), v(8, ZC), v(24, ZC), v(KH, 8, NY), v(512, NY), v(512, NY), v(512, NY), v(512, NY), v(512, NY),
            v(64, NY), v(192, NY), v(21, 8, NY), v(6, 8, NY),
            v(2, 6, 8, NY), v(4, 2, 8, NY), v(2, 2, 16, 3, 8, NY), v(2, 2, 4, 3, 8, NY), v(2, 2, 4, 3, 8, NY),
            v(2, 2, 8, 3, 8, NY), v(2, 8, 6, 8, NY), v(2, NX, NX), v(2, NX, NX), v(2, 2, NY, NY), v(6, 8, NY),
            v(2, 8 * NX, NY),
            v(ZC, 8, NY), v(8, KH, 8, NY), v(KH, NX, NY), v(KH, NX, NY), v(2, KH, 8, NY), v(KH, 8, NY),
            dma((7,)), dma((4,)), dma((4,)), dma((2, 2, 16)), dma((2, 2, 16)), dma((2, 2, 4)), dma((2, 2, 4)),
            dma((2, 2, 8)), dma((2, 2, 8)), dma((2, 8)), dma((2, 8)), dma((2, 8)), dma((2, 8)), dma((4,)), dma((4,)),
        ],
        compiler_params=pltpu.CompilerParams(collective_id=0, has_side_effects=True, vmem_limit_bytes=20 * 2**20),
    )(z_extent, lower_nbr, upper_nbr, *[
        pltpu.with_memory_space_constraint(a, pltpu.HBM)
        for a in (
            x_shift, y_shift,
            modes_now.reshape(slab * ZC, NY), modes_prev.reshape(slab * ZC, NY),
            jnp.asarray(cx), jnp.asarray(cx.T.copy()), cy,
        )
    ])
    anyw = pl.BlockSpec(memory_space=pl.ANY)
    outs = pl.pallas_call(
        finish,
        out_shape=(flat,) * 3,
        in_specs=[anyw, anyw, vmem, vmem, vmem],
        out_specs=(hbm,) * 3,
        scratch_shapes=[v(512, NY), dma((4,))],
        compiler_params=pltpu.CompilerParams(vmem_limit_bytes=8 * 2**20),
    )(nxt, cur, y, ztt, cy)
    return tuple(o.reshape(slab, ZC, NY) for o in outs)


def solution(mesh):
    placed = (
        P("split", "dom", None),
        P("split", "dom", None),
        P("dom"),
        P("dom"),
        P("dom"),
        P("dom", None),
        P("dom", None),
    )
    return jax.shard_map(
        on_device,
        mesh=mesh,
        in_specs=placed,
        out_specs=(P("split", "dom", None),) * 3,
        check_vma=False,
    )
```

time: 72 us -> 66.1 us (0.918)
  Pallas kernels: 69.2 us -> 63.3 us
    pallas_call x1, Pallas kernels: 67.9 us -> 62 us  [on_device(): pl.pallas_call(kernel, out_shape=(flat, flat, jax.ShapeDtypeStruct((2, KH...]
where the time goes in v3:
time: 66.1 us; the launch traced here: 65.9 us
  Pallas kernels  63.3 us (96%)
  between operations  2.59 us (4%)
    pallas_call x1, Pallas kernels, on_device(): pl.pallas_call(kernel, out_shape=(flat, flat, jax.ShapeDtypeStruct((2, KH...  62 us
    pallas_call x1, Pallas kernels, on_device(): pl.pallas_call(finish, out_shape=(flat,) * 3, in_specs=[anyw, anyw, vmem,...  1.36 us

profile of v3, /device:TPU:1, one launch (start us, length us, event | category | flops | bytes accessed | tf_op | source)
XLA Modules:
  0.0 65.9 jit_solution(6361364528577818340)
XLA Ops:
  2.6 0.0 copy-start
  2.6 62.0 %shard_map.121 = (f32[512,128]{1,0:T(8,128)S(1)}, f32[512,128]{1,0:T(8,128)S(1)}, f32[2,32,8,128]{3,2,1,0:T(8,128)S(1)}, f32[64,64]{1,0:T(8,128)S(1)}) custom-call(s32[1]{0:T(128)S(6)} %copy.13.ext, s32[1]{0:T(128)S(6)} %copy.14.low, s32[1]{0:T(128)S(6)} %copy.15.upp, s32[1,2]{1,0:T(1,128)} %xs_.1, s32[1,2]{1,0:T(1,128)} %ys_.1, f32[512,128]{1,0:T(8,128)} %bitcast.5, ...), custom_call_target="tpu_custom_call" | custom-call | tf_op jit(solution)/shard_map/pallas_call | solution.py:428
  64.6 0.0 copy-done
  64.6 1.4 %shard_map.122 = (f32[512,128]{1,0:T(8,128)}, f32[512,128]{1,0:T(8,128)}, f32[512,128]{1,0:T(8,128)}) custom-call(f32[512,128]{1,0:T(8,128)S(1)} %get-tuple-element.10.nxt_, f32[512,128]{1,0:T(8,128)S(1)} %get-tuple-element.11.cur_, f32[2,32,8,128]{3,2,1,0:T(8,128)S(1)} %get-tuple-element.12.y, f32[64,64]{1,0:T(8,128)S(1)} %get-tuple-element.13.ztt, ...), custom_call_target="tpu_custom_call" | custom-call | tf_op jit(solution)/shard_map/pallas_call | solution.py:454
Async XLA Ops:
  2.6 62.0 %copy-start = (f32[128,128]{1,0:T(8,128)S(1)}, f32[128,128]{1,0:T(8,128)}, u32[]{:S(2)}) copy-start(f32[128,128]{1,0:T(8,128)} %constant.6.clone.cy_.cy) | copy-start | bytes 196612

commit v4 on v3

--- a/solution.py
+++ b/solution.py
@@ -95,7 +95,7 @@
     def greet(d, s):
         pl.semaphore_signal(barrier, inc=1, device_id=(d, s), device_id_type=MESH)
 
-    for k in (2, 1, 3):
+    for k in (1, 3):
         greet(at(0, 4 * k), me)
     for i, d in GREET:
         greet(at(i, d), me)
@@ -133,7 +133,7 @@
         sscr[i * 8 : i * 8 + 8, :] = dot(rtt[...], m0[i * ZC : (i + 1) * ZC, :])
     for r in range(6):
         st[0, r] = sscr[pl.ds(r, 8, stride=8), :]
-    pl.semaphore_wait(barrier, len(GREET) + 3 + SN - 1)
+    pl.semaphore_wait(barrier, len(GREET) + 2 + SN - 1)
 
     def strip_rows(f):
         return slice(3, 6) if f == 0 else slice(0, 3)
@@ -147,7 +147,7 @@
                     near_s.at[step, f, n], near_r.at[step, f, n], at(i, d), me,
                 )
 
-    for k in (2, 1, 3):
+    for k in (1, 3):
         send(nb.at[0], nb.at[k], nb_s.at[k], nb_r.at[k], at(0, -4 * k), me)
     send_near(0)
 
@@ -178,20 +178,21 @@
         for t in range(1, SN):
             send(bb.at[step, me], bb.at[step, me], bb_s.at[step, t], bb_r.at[step, t], dom, other(t))
 
-    def to_far(step, f):
-        acc = [[jnp.zeros((8, NY), F32)] * 3 for _ in range(4)]
+    def to_far(step, f, ks, wait=True):
+        acc = {k: [jnp.zeros((8, NY), F32)] * 3 for k in ks}
         rows_f = strip_rows(f)
         for n, (i, d) in enumerate(WINDOWS[f]):
             if n == 0:
                 block = [st[step, r] for r in range(rows_f.start, rows_f.stop)]
             else:
-                arrived(near.at[step, f, n], near_s.at[step, f, n], near_r.at[step, f, n])
+                if wait:
+                    arrived(near.at[step, f, n], near_s.at[step, f, n], near_r.at[step, f, n])
                 block = [near[step, f, n, r] for r in range(3)]
             who = at(-i, -d).astype(F32)
-            for k in range(4):
+            for k in ks:
                 hit = nb[k, f] == who
                 acc[k] = [jnp.where(hit, v, a) for v, a in zip(block, acc[k])]
-        for k in (2, 1, 3, 0):
+        for k in ks:
             for r in range(3):
                 sel[step, f, k, r] = acc[k][r]
             if k:
@@ -254,10 +255,14 @@
         return 0
 
     lax.fori_loop(0, 8, bases, 0)
-    for k in (1, 3, 2):
-        arrived(nb.at[k], nb_s.at[k], nb_r.at[k])
-    to_far(0, 0)
-    to_far(0, 1)
+    arrived(nb.at[1], nb_s.at[1], nb_r.at[1])
+    send(nb.at[1], nb.at[2], nb_s.at[2], nb_r.at[2], at(0, -4), me)
+    arrived(nb.at[3], nb_s.at[3], nb_r.at[3])
+    to_far(0, 0, (1, 3, 0))
+    to_far(0, 1, (1, 3, 0))
+    arrived(nb.at[2], nb_s.at[2], nb_r.at[2])
+    to_far(0, 0, (2,), False)
+    to_far(0, 1, (2,), False)
 
     def turn(k, _):
         hs[k] = h0[pl.ds(k, 8, stride=ZC), :]
@@ -336,8 +341,8 @@
 
     arrived_h(0)
     lax.fori_loop(0, 16, early, 0)
-    to_far(1, 0)
-    to_far(1, 1)
+    to_far(1, 0, (2, 1, 3, 0))
+    to_far(1, 1, (2, 1, 3, 0))
 
     def step_one(i, _):
         m = b1[rows(i), :] + forced(0, i)

time: 66.1 us -> 67 us (1.014)
  Pallas kernels: 63.3 us -> 64.2 us
    pallas_call x1, Pallas kernels: 62 us -> 62.8 us  [on_device(): pl.pallas_call(kernel, out_shape=(flat, flat, jax.ShapeDtypeStruct((2, KH...]
where the time goes in v4:
time: 67 us; the launch traced here: 66.8 us
  Pallas kernels  64.2 us (96%)
  between operations  2.59 us (4%)
    pallas_call x1, Pallas kernels, on_device(): pl.pallas_call(kernel, out_shape=(flat, flat, jax.ShapeDtypeStruct((2, KH...  62.8 us
    pallas_call x1, Pallas kernels, on_device(): pl.pallas_call(finish, out_shape=(flat,) * 3, in_specs=[anyw, anyw, vmem,...  1.36 us

profile of v4, /device:TPU:1, one launch (start us, length us, event | category | flops | bytes accessed | tf_op | source)
XLA Modules:
  0.0 66.8 jit_solution(12038171241868752194)
XLA Ops:
  2.6 0.0 copy-start
  2.6 62.8 %shard_map.121 = (f32[512,128]{1,0:T(8,128)S(1)}, f32[512,128]{1,0:T(8,128)S(1)}, f32[2,32,8,128]{3,2,1,0:T(8,128)S(1)}, f32[64,64]{1,0:T(8,128)S(1)}) custom-call(s32[1]{0:T(128)S(6)} %copy.13.ext, s32[1]{0:T(128)S(6)} %copy.14.low, s32[1]{0:T(128)S(6)} %copy.15.upp, s32[1,2]{1,0:T(1,128)} %xs_.1, s32[1,2]{1,0:T(1,128)} %ys_.1, f32[512,128]{1,0:T(8,128)} %bitcast.5, ...), custom_call_target="tpu_custom_call" | custom-call | tf_op jit(solution)/shard_map/pallas_call | solution.py:433
  65.4 0.0 copy-done
  65.4 1.4 %shard_map.122 = (f32[512,128]{1,0:T(8,128)}, f32[512,128]{1,0:T(8,128)}, f32[512,128]{1,0:T(8,128)}) custom-call(f32[512,128]{1,0:T(8,128)S(1)} %get-tuple-element.10.nxt_, f32[512,128]{1,0:T(8,128)S(1)} %get-tuple-element.11.cur_, f32[2,32,8,128]{3,2,1,0:T(8,128)S(1)} %get-tuple-element.12.y, f32[64,64]{1,0:T(8,128)S(1)} %get-tuple-element.13.ztt, ...), custom_call_target="tpu_custom_call" | custom-call | tf_op jit(solution)/shard_map/pallas_call | solution.py:459
Async XLA Ops:
  2.6 62.8 %copy-start = (f32[128,128]{1,0:T(8,128)S(1)}, f32[128,128]{1,0:T(8,128)}, u32[]{:S(2)}) copy-start(f32[128,128]{1,0:T(8,128)} %constant.6.clone.cy_.cy) | copy-start | bytes 196612

commit v5 on v3

--- a/solution.py
+++ b/solution.py
@@ -62,7 +62,6 @@
     for ds in (range(-1, 3), range(-2, 2))
 ]
 GREET = [(i, d) for d in (-2, 2, -1, 1, 0) for i in (2, 1, 3, 0) if (i, d) != (0, 0)]
-KH = ZC // 2
 
 
 def kernel(
@@ -70,12 +69,11 @@
     nxt, cur, out, ztt,
     xs, ys, m0, m1, cx, cxt, cy,
     rt, rtt, w2, rtb, mz, b1, gn, h0, base2, sscr, kscr, kt, sb, st, nb, near, sel, far, aa, bb, xa, xb, yab, gb, g,
-    hs, hb, e1, ge, yo, yr,
+    hs, hb, ge, e0, yo, yr,
     in_s, nb_s, nb_r, near_s, near_r, far_s, far_r, aa_s, aa_r, bb_s, bb_r, h_s, h_r, y_s, y_r,
 ):
     dom, me = lax.axis_index("dom"), lax.axis_index("split")
     px, pz = dom // ZN, lax.rem(dom, ZN)
-    chip, core = me // 2, lax.rem(me, 2)
 
     loads = [
         pltpu.make_async_copy(a, b, in_s.at[n])
@@ -103,6 +101,11 @@
         greet(dom, other(t))
 
     started = []
+
+    def drained():
+        while started:
+            started.pop(0).wait_send()
+
 
     def send(src, dst, ss, rs, d, s):
         c = pltpu.make_async_remote_copy(
@@ -265,15 +268,9 @@
 
     lax.fori_loop(0, ZC, turn, 0, unroll=8)
 
-    def send_h(part):
-        for t in range(1, SN):
-            first = pl.multiple_of(lax.rem(other(t), 2) * KH + part * 16, 16)
-            send(
-                hs.at[pl.ds(first, 16)], hb.at[me, rows(part, 16)], h_s.at[part, t], h_r.at[part, t], dom, other(t)
-            )
-
-    send_h(0)
-    hb[me] = hs[rows(core, KH)]
+    for t in range(1, SN):
+        send(hs.at[rows(other(t), 8)], hb.at[me], h_s.at[t], h_r.at[t], dom, other(t))
+    hb[me] = hs[rows(me, 8)]
     for n, (a, b) in enumerate(PAIRS):
         w2[n : n + 1, :] = rtt[a : a + 1, :] * rtt[b : b + 1, :]
     w2[21:24, :] = jnp.zeros((3, ZC), F32)
@@ -288,6 +285,17 @@
         sb[r] = sscr[pl.ds(r, 8, stride=8), :]
     for n in range(21):
         kt[n] = kscr[pl.ds(n, 8, stride=24), :]
+    kx2 = (iota((NX, NY), 0) / NX) ** 2 + (iota((NX, NY), 1) / NY) ** 2
+
+    def angles(k):
+        z = jnp.full((NX, NY), k.astype(F32)) / lv
+        return HALF_PI_2 * (kx2 + z * z)
+
+    def gains(k, _):
+        ge[k] = gain_of(angles(k))
+        return 0
+
+    lax.fori_loop(0, ZC, gains, 0)
     gathered_own(0)
     for r in range(6):
         gb[r] = dot(xb[r // 3, rows(me, 8), :], ours(0, r))
@@ -309,33 +317,27 @@
         st[1, r] = s
     send_near(1)
     own_part(1)
-    send_h(1)
     for step in range(2):
         g[step, 6 * NX :, :] = jnp.zeros((2 * NX, NY), F32)
     for r in range(6):
         g[0, r * NX : (r + 1) * NX, :] = dot(xb[r // 3], ours(0, r)) + dot(xa[r // 3], theirs(0, r))
-    shape = (KH, 8, NY)
-    rtb[...] = row_table(iota(shape, 0) + (core * KH).astype(F32), iota(shape, 1))
-
-    kx2 = (iota((NX, NY), 0) / NX) ** 2 + (iota((NX, NY), 1) / NY) ** 2
+    shape = (ZC, 8, NY)
+    rtb[...] = row_table(iota(shape, 0), iota(shape, 1))
+    for t in range(1, SN):
+        arrived(hb.at[other(SN - t)], h_s.at[t], h_r.at[t])
+    loads[6].wait()
 
     def early(j, _):
-        z = jnp.full((NX, NY), (core * KH + j).astype(F32)) / lv
-        u = HALF_PI_2 * (kx2 + z * z)
-        gain = gain_of(u)
-        total = rtb[j, 0:1, :] * g[0, 0:NX, :]
+        k = me * 8 + j
+        gain = ge[k]
+        total = rtb[k, 0:1, :] * g[0, 0:NX, :]
         for r in range(1, 6):
-            total = total + rtb[j, r : r + 1, :] * g[0, r * NX : (r + 1) * NX, :]
-        ge[j] = gain
-        e1[j] = hb[:, j].reshape(NX, NY) + gain * (2.0 - u * gain) * total
-        return 0
-
-    def arrived_h(part):
-        for t in range(1, SN):
-            arrived(hb.at[other(SN - t), rows(part, 16)], h_s.at[part, t], h_r.at[part, t])
-
-    arrived_h(0)
-    lax.fori_loop(0, 16, early, 0)
+            total = total + rtb[k, r : r + 1, :] * g[0, r * NX : (r + 1) * NX, :]
+        e = hb[:, j].reshape(NX, NY) + gain * (2.0 - angles(k) * gain) * total
+        yo[:, j] = dot(cxt[...], e).reshape(SN, 8, NY)
+        return 0
+
+    lax.fori_loop(0, 8, early, 0)
     to_far(1, 0)
     to_far(1, 1)
 
@@ -345,56 +347,68 @@
         base2[rows(i), :] = (2.0 - twice(i) * gn[rows(i), :]) * m - mz[rows(i), :]
         return 0
 
+    drained()
+    for t in range(1, SN):
+        send(yo.at[other(t)], yr.at[rows(me, 8)], y_s.at[t], y_r.at[t], dom, other(t))
+    yr[rows(me, 8)] = yo[me]
     gathered_own(1)
     for r in range(6):
         g[1, r * NX : (r + 1) * NX, :] = dot(xb[r // 3], ours(1, r))
-    arrived_h(1)
-    lax.fori_loop(16, KH, early, 0)
-    loads[6].wait()
+    lax.fori_loop(0, 8, step_one, 0)
+    for t in range(1, SN):
+        arrived(yr.at[rows(other(SN - t), 8)], y_s.at[t], y_r.at[t])
     from_far(1, 0)
     from_far(1, 1)
-    lax.fori_loop(0, 8, step_one, 0)
-    for f in range(2):
+    drained()
+
+    def face(f):
         gathered(1, f)
         for r in range(3 * f, 3 * f + 3):
             g[1, r * NX : (r + 1) * NX, :] += dot(xa[f], theirs(1, r))
 
-    twin = 1 - core
-    cx16 = cxt[rows(chip, 16), :]
-    for part in range(4):
+    def weights(k, f):
+        return [jnp.broadcast_to(rtb[k, 3 * f + r : 3 * f + r + 1, :], (8, NY)) for r in range(3)]
+
+    def sources(f, x):
+        return [g[1, r * NX + x * 8 : r * NX + x * 8 + 8, :] for r in range(3 * f, 3 * f + 3)]
+
+    face(0)
+
+    def lower_part(i, _):
+        ws = [weights(i * 4 + n, 0) for n in range(4)]
+        for x in range(8):
+            src = sources(0, x)
+            for n, w in enumerate(ws):
+                e0[i * 4 + n, x * 8 : x * 8 + 8, :] = w[0] * src[0] + w[1] * src[1] + w[2] * src[2]
+        return 0
+
+    lax.fori_loop(0, ZC // 4, lower_part, 0)
+    face(1)
+    cx8 = cxt[rows(me, 8), :]
+    for i in range(8):
+        nxt[i * ZC : (i + 1) * ZC, :] = base2[i * ZC : (i + 1) * ZC, :] + forced(1, i)
+
+    def late(i, _):
         parts = []
-        for j in range(part * 8, part * 8 + 8, 2):
-            weights = [[jnp.broadcast_to(rtb[jj, r : r + 1, :], (8, NY)) for r in range(6)] for jj in (j, j + 1)]
-            tiles = [[], []]
+        for j in range(0, 8, 4):
+            ws = [weights(i * 8 + j + n, 1) for n in range(4)]
+            tiles = [[] for _ in ws]
             for x in range(8):
-                src = [g[1, r * NX + x * 8 : r * NX + x * 8 + 8, :] for r in range(6)]
-                for n in range(2):
-                    total = weights[n][0] * src[0]
-                    for r in range(1, 6):
-                        total = total + weights[n][r] * src[r]
-                    at_x = slice(x * 8, x * 8 + 8)
-                    tiles[n].append(e1[j + n, at_x, :] + ge[j + n, at_x, :] * total)
+                src = sources(1, x)
+                at_x = slice(x * 8, x * 8 + 8)
+                for n, w in enumerate(ws):
+                    k = i * 8 + j + n
+                    total = e0[k, at_x, :] + w[0] * src[0] + w[1] * src[1] + w[2] * src[2]
+                    tiles[n].append(ge[k, at_x, :] * total)
             parts += [jnp.concatenate(t, axis=0) for t in tiles]
-        x = dot(cx16, jnp.concatenate(parts, axis=1))
-        for c in range(2):
-            for j in range(8):
-                yo[c, part * 8 + j] = x[c * 8 : c * 8 + 8, j * NY : (j + 1) * NY]
-        p8 = rows(part, 8)
-        send(yo.at[twin, p8], yr.at[p8], y_s.at[part], y_r.at[part], dom, chip * 2 + twin)
-
-    def step_two(i, _):
-        nxt[rows(i), :] = base2[rows(i), :] + forced(1, i)
-        return 0
-
-    lax.fori_loop(0, 8, step_two, 0)
-    out[core] = yo[core]
-    for part in range(4):
-        p8 = rows(part, 8)
-        arrived(yr.at[p8], y_s.at[part], y_r.at[part])
-        out[twin, p8] = yr[p8]
-
-    for c in started:
-        c.wait_send()
+        x = dot(cx8, jnp.concatenate(parts, axis=1))
+        for j in range(8):
+            out[i * 8 + j] = yr[i * 8 + j] + x[:, j * NY : (j + 1) * NY]
+        return 0
+
+    for i in range(8):
+        late(i, 0)
+    drained()
 
 
 def finish(nxt_, cur_, y, ztt, cy, nxt, cur, prs, p, sems):
@@ -402,7 +416,7 @@
     for c in copies:
         c.start()
     for h in range(2):
-        a = dot(ztt[...], jnp.concatenate([y[:, :, i].reshape(ZC, NY) for i in range(h * 4, h * 4 + 4)], axis=1))
+        a = dot(ztt[...], jnp.concatenate([y[:, i, :] for i in range(h * 4, h * 4 + 4)], axis=1))
         a = jnp.concatenate([a[:, n * NY : (n + 1) * NY] for n in range(4)], axis=0)
         p[h * 4 * ZC : (h + 1) * 4 * ZC, :] = dot(a, cy[...])
         c = pltpu.make_async_copy(p.at[rows(h, 4 * ZC)], prs.at[rows(h, 4 * ZC)], sems.at[2 + h])
@@ -427,19 +441,19 @@
     dma = pltpu.SemaphoreType.DMA
     nxt, cur, y, ztt = pl.pallas_call(
         kernel,
-        out_shape=(flat, flat, jax.ShapeDtypeStruct((2, KH, 8, NY), F32), jax.ShapeDtypeStruct((ZC, ZC), F32)),
+        out_shape=(flat, flat, jax.ShapeDtypeStruct((ZC, 8, NY), F32), jax.ShapeDtypeStruct((ZC, ZC), F32)),
         in_specs=[pl.BlockSpec(memory_space=pltpu.SMEM)] * 3 + [hbm] * 7,
         out_specs=(vmem,) * 4,
         scratch_shapes=[
             sm(1, 2), sm(1, 2), v(512, NY), v(512, NY), v(NX, NX), v(NX, NX), v(NY, NY),
-            v(ZC, 8), v(8, ZC), v(24, ZC), v(KH, 8, NY), v(512, NY), v(512, NY), v(512, NY), v(512, NY), v(512, NY),
+            v(ZC, 8), v(8, ZC), v(24, ZC), v(ZC, 8, NY), v(512, NY), v(512, NY), v(512, NY), v(512, NY), v(512, NY),
             v(64, NY), v(192, NY), v(21, 8, NY), v(6, 8, NY),
             v(2, 6, 8, NY), v(4, 2, 8, NY), v(2, 2, 16, 3, 8, NY), v(2, 2, 4, 3, 8, NY), v(2, 2, 4, 3, 8, NY),
             v(2, 2, 8, 3, 8, NY), v(2, 8, 6, 8, NY), v(2, NX, NX), v(2, NX, NX), v(2, 2, NY, NY), v(6, 8, NY),
             v(2, 8 * NX, NY),
-            v(ZC, 8, NY), v(8, KH, 8, NY), v(KH, NX, NY), v(KH, NX, NY), v(2, KH, 8, NY), v(KH, 8, NY),
+            v(ZC, 8, NY), v(8, 8, 8, NY), v(ZC, NX, NY), v(ZC, NX, NY), v(8, 8, 8, NY), v(ZC, 8, NY),
             dma((7,)), dma((4,)), dma((4,)), dma((2, 2, 16)), dma((2, 2, 16)), dma((2, 2, 4)), dma((2, 2, 4)),
-            dma((2, 2, 8)), dma((2, 2, 8)), dma((2, 8)), dma((2, 8)), dma((2, 8)), dma((2, 8)), dma((4,)), dma((4,)),
+            dma((2, 2, 8)), dma((2, 2, 8)), dma((2, 8)), dma((2, 8)), dma((8,)), dma((8,)), dma((8,)), dma((8,)),
         ],
         compiler_params=pltpu.CompilerParams(collective_id=0, has_side_effects=True, vmem_limit_bytes=20 * 2**20),
     )(z_extent, lower_nbr, upper_nbr, *[

time: 66.1 us -> 64.5 us (0.976)
  Pallas kernels: 63.3 us -> 61.7 us
    pallas_call x1, Pallas kernels: 62 us -> 60.4 us  [on_device(): pl.pallas_call(kernel, out_shape=(flat, flat, jax.ShapeDtypeStruct((ZC, 8...]
where the time goes in v5:
time: 64.5 us; the launch traced here: 64.3 us
  Pallas kernels  61.7 us (96%)
  between operations  2.59 us (4%)
    pallas_call x1, Pallas kernels, on_device(): pl.pallas_call(kernel, out_shape=(flat, flat, jax.ShapeDtypeStruct((ZC, 8...  60.4 us
    pallas_call x1, Pallas kernels, on_device(): pl.pallas_call(finish, out_shape=(flat,) * 3, in_specs=[anyw, anyw, vmem,...  1.36 us

profile of v5, /device:TPU:1, one launch (start us, length us, event | category | flops | bytes accessed | tf_op | source)
XLA Modules:
  0.0 64.3 jit_solution(3134309227306987102)
XLA Ops:
  2.6 0.0 copy-start
  2.6 60.4 %shard_map.121 = (f32[512,128]{1,0:T(8,128)S(1)}, f32[512,128]{1,0:T(8,128)S(1)}, f32[64,8,128]{2,1,0:T(8,128)S(1)}, f32[64,64]{1,0:T(8,128)S(1)}) custom-call(s32[1]{0:T(128)S(6)} %copy.13.ext, s32[1]{0:T(128)S(6)} %copy.14.low, s32[1]{0:T(128)S(6)} %copy.15.upp, s32[1,2]{1,0:T(1,128)} %xs_.1, s32[1,2]{1,0:T(1,128)} %ys_.1, f32[512,128]{1,0:T(8,128)} %bitcast.5, ...), custom_call_target="tpu_custom_call" | custom-call | tf_op jit(solution)/shard_map/pallas_call | solution.py:442
  63.0 0.0 copy-done
  63.0 1.4 %shard_map.122 = (f32[512,128]{1,0:T(8,128)}, f32[512,128]{1,0:T(8,128)}, f32[512,128]{1,0:T(8,128)}) custom-call(f32[512,128]{1,0:T(8,128)S(1)} %get-tuple-element.10.nxt_, f32[512,128]{1,0:T(8,128)S(1)} %get-tuple-element.11.cur_, f32[64,8,128]{2,1,0:T(8,128)S(1)} %get-tuple-element.12.y, f32[64,64]{1,0:T(8,128)S(1)} %get-tuple-element.13.ztt, ...), custom_call_target="tpu_custom_call" | custom-call | tf_op jit(solution)/shard_map/pallas_call | solution.py:468
Async XLA Ops:
  2.6 60.4 %copy-start = (f32[128,128]{1,0:T(8,128)S(1)}, f32[128,128]{1,0:T(8,128)}, u32[]{:S(2)}) copy-start(f32[128,128]{1,0:T(8,128)} %constant.6.clone.cy_.cy) | copy-start | bytes 196612

commit v6 on v5

--- a/solution.py
+++ b/solution.py
@@ -102,22 +102,33 @@
 
     started = []
 
+    def send(src, dst, ss, rs, d, s):
+        pltpu.make_async_remote_copy(
+            src_ref=src, dst_ref=dst, send_sem=ss, recv_sem=rs, device_id=(d, s), device_id_type=MESH
+        ).start()
+
+    def group(whole, ss, rs):
+        return pltpu.make_async_remote_copy(
+            src_ref=whole, dst_ref=whole, send_sem=ss, recv_sem=rs, device_id=(dom, me), device_id_type=MESH
+        )
+
+    def near_group(step, f):
+        return group(near.at[step, f, 1:16], near_s.at[step, f], near_r.at[step, f])
+
+    def far_group(step, f):
+        return group(far.at[step, f, 1:4], far_s.at[step, f], far_r.at[step, f])
+
+    def aa_group(step, f):
+        return group(aa.at[step, f, 0:7], aa_s.at[step, f], aa_r.at[step, f])
+
+    def bb_group(step):
+        return group(bb.at[step, 0:7], bb_s.at[step], bb_r.at[step])
+
+    nb_group, h_group, y_group = group(nb.at[1:4], nb_s, nb_r), group(hb.at[0:7], h_s, h_r), group(yr.at[0:56], y_s, y_r)
+
     def drained():
         while started:
             started.pop(0).wait_send()
-
-
-    def send(src, dst, ss, rs, d, s):
-        c = pltpu.make_async_remote_copy(
-            src_ref=src, dst_ref=dst, send_sem=ss, recv_sem=rs, device_id=(d, s), device_id_type=MESH
-        )
-        c.start()
-        started.append(c)
-
-    def arrived(dst, ss, rs):
-        pltpu.make_async_remote_copy(
-            src_ref=dst, dst_ref=dst, send_sem=ss, recv_sem=rs, device_id=(dom, me), device_id_type=MESH
-        ).wait_recv()
 
     length = ext[0].astype(F32)
 
@@ -145,13 +156,12 @@
         for f in range(2):
             for n in range(15, 0, -1):
                 i, d = WINDOWS[f][n]
-                send(
-                    st.at[step, strip_rows(f)], near.at[step, f, n],
-                    near_s.at[step, f, n], near_r.at[step, f, n], at(i, d), me,
-                )
+                send(st.at[step, strip_rows(f)], near.at[step, f, n], near_s.at[step, f], near_r.at[step, f], at(i, d), me)
+            started.append(near_group(step, f))
 
     for k in (2, 1, 3):
-        send(nb.at[0], nb.at[k], nb_s.at[k], nb_r.at[k], at(0, -4 * k), me)
+        send(nb.at[0], nb.at[k], nb_s, nb_r, at(0, -4 * k), me)
+    started.append(nb_group)
     send_near(0)
 
     for c in loads[1:5]:
@@ -179,16 +189,17 @@
         for f, part in enumerate((low_rows(p[0], p[1], p[2]), low_rows(p[5], p[4], p[3])[::-1])):
             bb[step, me, 3 * f : 3 * f + 3] = dot(jnp.concatenate(part, axis=0), yab[f, 1]).reshape(3, 8, NY)
         for t in range(1, SN):
-            send(bb.at[step, me], bb.at[step, me], bb_s.at[step, t], bb_r.at[step, t], dom, other(t))
+            send(bb.at[step, me], bb.at[step, me], bb_s.at[step], bb_r.at[step], dom, other(t))
+        started.append(bb_group(step))
 
     def to_far(step, f):
         acc = [[jnp.zeros((8, NY), F32)] * 3 for _ in range(4)]
         rows_f = strip_rows(f)
+        near_group(step, f).wait_recv()
         for n, (i, d) in enumerate(WINDOWS[f]):
             if n == 0:
                 block = [st[step, r] for r in range(rows_f.start, rows_f.stop)]
             else:
-                arrived(near.at[step, f, n], near_s.at[step, f, n], near_r.at[step, f, n])
                 block = [near[step, f, n, r] for r in range(3)]
             who = at(-i, -d).astype(F32)
             for k in range(4):
@@ -198,28 +209,19 @@
             for r in range(3):
                 sel[step, f, k, r] = acc[k][r]
             if k:
-                send(
-                    sel.at[step, f, k], far.at[step, f, k],
-                    far_s.at[step, f, k], far_r.at[step, f, k], at(0, 4 * k), me,
-                )
+                send(sel.at[step, f, k], far.at[step, f, k], far_s.at[step, f], far_r.at[step, f], at(0, 4 * k), me)
+        started.append(far_group(step, f))
 
     def from_far(step, f):
         q = [sel[step, f, 0, r] for r in range(3)]
+        far_group(step, f).wait_recv()
         for k in (1, 3, 2):
-            arrived(far.at[step, f, k], far_s.at[step, f, k], far_r.at[step, f, k])
             q = [a + far[step, f, k, r] for r, a in enumerate(q)]
         part = low_rows(*q)[::-1] if f else low_rows(*q[::-1])
         aa[step, f, me] = dot(jnp.concatenate(part, axis=0), yab[f, 0]).reshape(3, 8, NY)
         for t in range(1, SN):
-            send(aa.at[step, f, me], aa.at[step, f, me], aa_s.at[step, f, t], aa_r.at[step, f, t], dom, other(t))
-
-    def gathered_own(step):
-        for t in range(1, SN):
-            arrived(bb.at[step, other(SN - t)], bb_s.at[step, t], bb_r.at[step, t])
-
-    def gathered(step, f):
-        for t in range(1, SN):
-            arrived(aa.at[step, f, other(SN - t)], aa_s.at[step, f, t], aa_r.at[step, f, t])
+            send(aa.at[step, f, me], aa.at[step, f, me], aa_s.at[step, f], aa_r.at[step, f], dom, other(t))
+        started.append(aa_group(step, f))
 
     def theirs(step, r):
         return aa[step, r // 3, :, r % 3].reshape(NX, NY)
@@ -257,8 +259,7 @@
         return 0
 
     lax.fori_loop(0, 8, bases, 0)
-    for k in (1, 3, 2):
-        arrived(nb.at[k], nb_s.at[k], nb_r.at[k])
+    nb_group.wait_recv()
     to_far(0, 0)
     to_far(0, 1)
 
@@ -269,7 +270,8 @@
     lax.fori_loop(0, ZC, turn, 0, unroll=8)
 
     for t in range(1, SN):
-        send(hs.at[rows(other(t), 8)], hb.at[me], h_s.at[t], h_r.at[t], dom, other(t))
+        send(hs.at[rows(other(t), 8)], hb.at[me], h_s, h_r, dom, other(t))
+    started.append(h_group)
     hb[me] = hs[rows(me, 8)]
     for n, (a, b) in enumerate(PAIRS):
         w2[n : n + 1, :] = rtt[a : a + 1, :] * rtt[b : b + 1, :]
@@ -296,7 +298,7 @@
         return 0
 
     lax.fori_loop(0, ZC, gains, 0)
-    gathered_own(0)
+    bb_group(0).wait_recv()
     for r in range(6):
         gb[r] = dot(xb[r // 3, rows(me, 8), :], ours(0, r))
     from_far(0, 0)
@@ -307,7 +309,7 @@
     ztt[...] = jnp.where((kk < length) & (zz < length), cos_table(kk, zz, jnp.full((ZC, ZC), length)), 0.0)
     g1 = []
     for f in range(2):
-        gathered(0, f)
+        aa_group(0, f).wait_recv()
         for r in range(3 * f, 3 * f + 3):
             g1.append(gb[r] + dot(xa[f, rows(me, 8), :], theirs(0, r)))
     for r in range(6):
@@ -323,8 +325,7 @@
         g[0, r * NX : (r + 1) * NX, :] = dot(xb[r // 3], ours(0, r)) + dot(xa[r // 3], theirs(0, r))
     shape = (ZC, 8, NY)
     rtb[...] = row_table(iota(shape, 0), iota(shape, 1))
-    for t in range(1, SN):
-        arrived(hb.at[other(SN - t)], h_s.at[t], h_r.at[t])
+    h_group.wait_recv()
     loads[6].wait()
 
     def early(j, _):
@@ -349,20 +350,20 @@
 
     drained()
     for t in range(1, SN):
-        send(yo.at[other(t)], yr.at[rows(me, 8)], y_s.at[t], y_r.at[t], dom, other(t))
+        send(yo.at[other(t)], yr.at[rows(me, 8)], y_s, y_r, dom, other(t))
+    started.append(y_group)
     yr[rows(me, 8)] = yo[me]
-    gathered_own(1)
+    bb_group(1).wait_recv()
     for r in range(6):
         g[1, r * NX : (r + 1) * NX, :] = dot(xb[r // 3], ours(1, r))
     lax.fori_loop(0, 8, step_one, 0)
-    for t in range(1, SN):
-        arrived(yr.at[rows(other(SN - t), 8)], y_s.at[t], y_r.at[t])
+    y_group.wait_recv()
     from_far(1, 0)
     from_far(1, 1)
     drained()
 
     def face(f):
-        gathered(1, f)
+        aa_group(1, f).wait_recv()
         for r in range(3 * f, 3 * f + 3):
             g[1, r * NX : (r + 1) * NX, :] += dot(xa[f], theirs(1, r))
 
@@ -452,8 +453,8 @@
             v(2, 2, 8, 3, 8, NY), v(2, 8, 6, 8, NY), v(2, NX, NX), v(2, NX, NX), v(2, 2, NY, NY), v(6, 8, NY),
             v(2, 8 * NX, NY),
             v(ZC, 8, NY), v(8, 8, 8, NY), v(ZC, NX, NY), v(ZC, NX, NY), v(8, 8, 8, NY), v(ZC, 8, NY),
-            dma((7,)), dma((4,)), dma((4,)), dma((2, 2, 16)), dma((2, 2, 16)), dma((2, 2, 4)), dma((2, 2, 4)),
-            dma((2, 2, 8)), dma((2, 2, 8)), dma((2, 8)), dma((2, 8)), dma((8,)), dma((8,)), dma((8,)), dma((8,)),
+            dma((7,)), dma, dma, dma((2, 2)), dma((2, 2)), dma((2, 2)), dma((2, 2)),
+            dma((2, 2)), dma((2, 2)), dma((2,)), dma((2,)), dma, dma, dma, dma,
         ],
         compiler_params=pltpu.CompilerParams(collective_id=0, has_side_effects=True, vmem_limit_bytes=20 * 2**20),
     )(z_extent, lower_nbr, upper_nbr, *[

time: 64.5 us -> 62.3 us (0.966)
  Pallas kernels: 61.7 us -> 59.5 us
    pallas_call x1, Pallas kernels: 60.4 us -> 58.1 us  [on_device(): pl.pallas_call(kernel, out_shape=(flat, flat, jax.ShapeDtypeStruct((ZC, 8...]
where the time goes in v6:
time: 62.3 us; the launch traced here: 62.1 us
  Pallas kernels  59.5 us (96%)
  between operations  2.59 us (4%)
    pallas_call x1, Pallas kernels, on_device(): pl.pallas_call(kernel, out_shape=(flat, flat, jax.ShapeDtypeStruct((ZC, 8...  58.1 us
    pallas_call x1, Pallas kernels, on_device(): pl.pallas_call(finish, out_shape=(flat,) * 3, in_specs=[anyw, anyw, vmem,...  1.36 us

profile of v6, /device:TPU:1, one launch (start us, length us, event | category | flops | bytes accessed | tf_op | source)
XLA Modules:
  0.0 62.1 jit_solution(7375356674708038355)
XLA Ops:
  2.6 0.0 copy-start
  2.6 58.1 %shard_map.121 = (f32[512,128]{1,0:T(8,128)S(1)}, f32[512,128]{1,0:T(8,128)S(1)}, f32[64,8,128]{2,1,0:T(8,128)S(1)}, f32[64,64]{1,0:T(8,128)S(1)}) custom-call(s32[1]{0:T(128)S(6)} %copy.13.ext, s32[1]{0:T(128)S(6)} %copy.14.low, s32[1]{0:T(128)S(6)} %copy.15.upp, s32[1,2]{1,0:T(1,128)} %xs_.1, s32[1,2]{1,0:T(1,128)} %ys_.1, f32[512,128]{1,0:T(8,128)} %bitcast.5, ...), custom_call_target="tpu_custom_call" | custom-call | tf_op jit(solution)/shard_map/pallas_call | solution.py:443
  60.7 0.0 copy-done
  60.7 1.4 %shard_map.122 = (f32[512,128]{1,0:T(8,128)}, f32[512,128]{1,0:T(8,128)}, f32[512,128]{1,0:T(8,128)}) custom-call(f32[512,128]{1,0:T(8,128)S(1)} %get-tuple-element.10.nxt_, f32[512,128]{1,0:T(8,128)S(1)} %get-tuple-element.11.cur_, f32[64,8,128]{2,1,0:T(8,128)S(1)} %get-tuple-element.12.y, f32[64,64]{1,0:T(8,128)S(1)} %get-tuple-element.13.ztt, ...), custom_call_target="tpu_custom_call" | custom-call | tf_op jit(solution)/shard_map/pallas_call | solution.py:469
Async XLA Ops:
  2.6 58.1 %copy-start = (f32[128,128]{1,0:T(8,128)S(1)}, f32[128,128]{1,0:T(8,128)}, u32[]{:S(2)}) copy-start(f32[128,128]{1,0:T(8,128)} %constant.6.clone.cy_.cy) | copy-start | bytes 196612

commit v7 on v6

--- a/solution.py
+++ b/solution.py
@@ -126,8 +126,8 @@
 
     nb_group, h_group, y_group = group(nb.at[1:4], nb_s, nb_r), group(hb.at[0:7], h_s, h_r), group(yr.at[0:56], y_s, y_r)
 
-    def drained():
-        while started:
+    def drained(keep=0):
+        while len(started) > keep:
             started.pop(0).wait_send()
 
     length = ext[0].astype(F32)
@@ -219,7 +219,7 @@
             q = [a + far[step, f, k, r] for r, a in enumerate(q)]
         part = low_rows(*q)[::-1] if f else low_rows(*q[::-1])
         aa[step, f, me] = dot(jnp.concatenate(part, axis=0), yab[f, 0]).reshape(3, 8, NY)
-        for t in range(1, SN):
+        for t in (4, 3, 5, 2, 6, 1, 7):
             send(aa.at[step, f, me], aa.at[step, f, me], aa_s.at[step, f], aa_r.at[step, f], dom, other(t))
         started.append(aa_group(step, f))
 
@@ -360,7 +360,7 @@
     y_group.wait_recv()
     from_far(1, 0)
     from_far(1, 1)
-    drained()
+    drained(2)
 
     def face(f):
         aa_group(1, f).wait_recv()
@@ -416,11 +416,11 @@
     copies = [pltpu.make_async_copy(nxt_, nxt, sems.at[0]), pltpu.make_async_copy(cur_, cur, sems.at[1])]
     for c in copies:
         c.start()
-    for h in range(2):
-        a = dot(ztt[...], jnp.concatenate([y[:, i, :] for i in range(h * 4, h * 4 + 4)], axis=1))
-        a = jnp.concatenate([a[:, n * NY : (n + 1) * NY] for n in range(4)], axis=0)
-        p[h * 4 * ZC : (h + 1) * 4 * ZC, :] = dot(a, cy[...])
-        c = pltpu.make_async_copy(p.at[rows(h, 4 * ZC)], prs.at[rows(h, 4 * ZC)], sems.at[2 + h])
+    for h in range(4):
+        a = dot(ztt[...], jnp.concatenate([y[:, i, :] for i in range(h * 2, h * 2 + 2)], axis=1))
+        a = jnp.concatenate([a[:, n * NY : (n + 1) * NY] for n in range(2)], axis=0)
+        p[h * 2 * ZC : (h + 1) * 2 * ZC, :] = dot(a, cy[...])
+        c = pltpu.make_async_copy(p.at[rows(h, 2 * ZC)], prs.at[rows(h, 2 * ZC)], sems.at[2 + h])
         c.start()
         copies.append(c)
     for c in copies:
@@ -471,7 +471,7 @@
         out_shape=(flat,) * 3,
         in_specs=[anyw, anyw, vmem, vmem, vmem],
         out_specs=(hbm,) * 3,
-        scratch_shapes=[v(512, NY), dma((4,))],
+        scratch_shapes=[v(512, NY), dma((6,))],
         compiler_params=pltpu.CompilerParams(vmem_limit_bytes=8 * 2**20),
     )(nxt, cur, y, ztt, cy)
     return tuple(o.reshape(slab, ZC, NY) for o in outs)

time: 62.3 us -> 61.7 us (level)
  no operation moved by 1% of the time
where the time goes in v7:
time: 61.7 us; the launch traced here: 61.5 us
  Pallas kernels  58.9 us (95%)
  between operations  2.59 us (4%)
    pallas_call x1, Pallas kernels, on_device(): pl.pallas_call(kernel, out_shape=(flat, flat, jax.ShapeDtypeStruct((ZC, 8...  57.7 us

profile of v7, /device:TPU:1, one launch (start us, length us, event | category | flops | bytes accessed | tf_op | source)
XLA Modules:
  0.0 61.5 jit_solution(18123819199844264259)
XLA Ops:
  2.6 0.0 copy-start
  2.6 57.7 %shard_map.121 = (f32[512,128]{1,0:T(8,128)S(1)}, f32[512,128]{1,0:T(8,128)S(1)}, f32[64,8,128]{2,1,0:T(8,128)S(1)}, f32[64,64]{1,0:T(8,128)S(1)}) custom-call(s32[1]{0:T(128)S(6)} %copy.13.ext, s32[1]{0:T(128)S(6)} %copy.14.low, s32[1]{0:T(128)S(6)} %copy.15.upp, s32[1,2]{1,0:T(1,128)} %xs_.1, s32[1,2]{1,0:T(1,128)} %ys_.1, f32[512,128]{1,0:T(8,128)} %bitcast.5, ...), custom_call_target="tpu_custom_call" | custom-call | tf_op jit(solution)/shard_map/pallas_call | solution.py:443
  60.3 0.0 copy-done
  60.3 1.2 %shard_map.122 = (f32[512,128]{1,0:T(8,128)}, f32[512,128]{1,0:T(8,128)}, f32[512,128]{1,0:T(8,128)}) custom-call(f32[512,128]{1,0:T(8,128)S(1)} %get-tuple-element.10.nxt_, f32[512,128]{1,0:T(8,128)S(1)} %get-tuple-element.11.cur_, f32[64,8,128]{2,1,0:T(8,128)S(1)} %get-tuple-element.12.y, f32[64,64]{1,0:T(8,128)S(1)} %get-tuple-element.13.ztt, ...), custom_call_target="tpu_custom_call" | custom-call | tf_op jit(solution)/shard_map/pallas_call | solution.py:469
Async XLA Ops:
  2.6 57.7 %copy-start = (f32[128,128]{1,0:T(8,128)S(1)}, f32[128,128]{1,0:T(8,128)}, u32[]{:S(2)}) copy-start(f32[128,128]{1,0:T(8,128)} %constant.6.clone.cy_.cy) | copy-start | bytes 196612

commit v8 on v7

--- a/solution.py
+++ b/solution.py
@@ -126,8 +126,8 @@
 
     nb_group, h_group, y_group = group(nb.at[1:4], nb_s, nb_r), group(hb.at[0:7], h_s, h_r), group(yr.at[0:56], y_s, y_r)
 
-    def drained(keep=0):
-        while len(started) > keep:
+    def drained():
+        while started:
             started.pop(0).wait_send()
 
     length = ext[0].astype(F32)
@@ -188,7 +188,7 @@
         p = [st[step, r] for r in range(6)]
         for f, part in enumerate((low_rows(p[0], p[1], p[2]), low_rows(p[5], p[4], p[3])[::-1])):
             bb[step, me, 3 * f : 3 * f + 3] = dot(jnp.concatenate(part, axis=0), yab[f, 1]).reshape(3, 8, NY)
-        for t in range(1, SN):
+        for t in (4, 3, 5, 2, 6, 1, 7):
             send(bb.at[step, me], bb.at[step, me], bb_s.at[step], bb_r.at[step], dom, other(t))
         started.append(bb_group(step))
 
@@ -269,7 +269,7 @@
 
     lax.fori_loop(0, ZC, turn, 0, unroll=8)
 
-    for t in range(1, SN):
+    for t in (4, 3, 5, 2, 6, 1, 7):
         send(hs.at[rows(other(t), 8)], hb.at[me], h_s, h_r, dom, other(t))
     started.append(h_group)
     hb[me] = hs[rows(me, 8)]
@@ -349,7 +349,7 @@
         return 0
 
     drained()
-    for t in range(1, SN):
+    for t in (4, 3, 5, 2, 6, 1, 7):
         send(yo.at[other(t)], yr.at[rows(me, 8)], y_s, y_r, dom, other(t))
     started.append(y_group)
     yr[rows(me, 8)] = yo[me]
@@ -360,7 +360,6 @@
     y_group.wait_recv()
     from_far(1, 0)
     from_far(1, 1)
-    drained(2)
 
     def face(f):
         aa_group(1, f).wait_recv()

time: 61.7 us -> 61.7 us (level)
  no operation moved by 1% of the time
where the time goes in v8:
time: 61.7 us; the launch traced here: 61.5 us
  Pallas kernels  58.9 us (95%)
  between operations  2.59 us (4%)
    pallas_call x1, Pallas kernels, on_device(): pl.pallas_call(kernel, out_shape=(flat, flat, jax.ShapeDtypeStruct((ZC, 8...  57.7 us

profile of v8, /device:TPU:1, one launch (start us, length us, event | category | flops | bytes accessed | tf_op | source)
XLA Modules:
  0.0 61.5 jit_solution(17719864883924947616)
XLA Ops:
  2.6 0.0 copy-start
  2.6 57.7 %shard_map.121 = (f32[512,128]{1,0:T(8,128)S(1)}, f32[512,128]{1,0:T(8,128)S(1)}, f32[64,8,128]{2,1,0:T(8,128)S(1)}, f32[64,64]{1,0:T(8,128)S(1)}) custom-call(s32[1]{0:T(128)S(6)} %copy.13.ext, s32[1]{0:T(128)S(6)} %copy.14.low, s32[1]{0:T(128)S(6)} %copy.15.upp, s32[1,2]{1,0:T(1,128)} %xs_.1, s32[1,2]{1,0:T(1,128)} %ys_.1, f32[512,128]{1,0:T(8,128)} %bitcast.5, ...), custom_call_target="tpu_custom_call" | custom-call | tf_op jit(solution)/shard_map/pallas_call | solution.py:442
  60.3 0.0 copy-done
  60.3 1.2 %shard_map.122 = (f32[512,128]{1,0:T(8,128)}, f32[512,128]{1,0:T(8,128)}, f32[512,128]{1,0:T(8,128)}) custom-call(f32[512,128]{1,0:T(8,128)S(1)} %get-tuple-element.10.nxt_, f32[512,128]{1,0:T(8,128)S(1)} %get-tuple-element.11.cur_, f32[64,8,128]{2,1,0:T(8,128)S(1)} %get-tuple-element.12.y, f32[64,64]{1,0:T(8,128)S(1)} %get-tuple-element.13.ztt, ...), custom_call_target="tpu_custom_call" | custom-call | tf_op jit(solution)/shard_map/pallas_call | solution.py:468
Async XLA Ops:
  2.6 57.7 %copy-start = (f32[128,128]{1,0:T(8,128)S(1)}, f32[128,128]{1,0:T(8,128)}, u32[]{:S(2)}) copy-start(f32[128,128]{1,0:T(8,128)} %constant.6.clone.cy_.cy) | copy-start | bytes 196612
